TPU v7x, 128 devices: a whole 4x4x4 slice. The times are simulated.
128 devices in a mesh: arc: 16 (over x, z), vec: 8 (over y, core).
Axes of the slice: x: 4, y: 4, z: 4, core: 2. Of those that a mesh axis runs over, the one named last changes fastest.
Arguments:
- right_side: float32 [640, 128, 128], P(('arc', 'vec')), may hold values from -6 to 6
- prior_diag: float32 [640, 128], P(('arc', 'vec')), may hold values from 0.5 to 4
- inv_factor: bfloat16 [2048, 256, 256], P(('arc', 'vec'))
- coupling_panel: bfloat16 [2048, 256, 1024], P(('arc', 'vec')), may hold values from -0.09375 to 0.09375
- coupling_owner: int32 [2048, 8], replicated, may hold values from 0 to 127, all different within a row; in each aligned block of 16 rows (0 to 15, 16 to 31, ...) at most 2 rows name the same one
- coupling_block: int32 [2048, 8], replicated, may hold values from 0 to 4
Outputs:
- solution_field: float32 [640, 128, 128], P(('arc', 'vec'))
- residual: float32 [640, 128, 128], P(('arc', 'vec'))
Inputs may be any that keep to these rules, and one draw needn't show every extreme that they name: `coupling_owner`: the 8 holders named for one arc are different. Among the 16 arcs of one device (aligned blocks of rows) no holder is named more than 2 times; some holder is named exactly 2 times.
All inputs are finite; a program needn't handle non-finite values.
Results may differ from a plain program's by a relative error of at most 0.006.
The roundings to bfloat16 on the way count: a program that leaves them out, or rounds other values in their place, can miss the bound.
Values may be sent and summed in bfloat16 or wider, within the bound.
A program may use at most 128 MiB of HBM per device.

v0:
```python
import jax
import jax.numpy as jnp
from jax import lax
from jax.sharding import PartitionSpec as P

ITERS = 2


def inner_gram(left, right):
    return jnp.einsum("grc,grd->cd", left, right, precision=lax.Precision.HIGHEST)


def combine_cols(field, weights):
    return jnp.einsum("grc,cd->grd", field, weights, precision=lax.Precision.HIGHEST)


def trade_out(buffer):
    return lax.all_to_all(buffer, ("arc", "vec"), split_axis=0, concat_axis=0, tiled=True)


def trade_back(buffer):
    return lax.all_to_all(buffer, ("arc", "vec"), split_axis=0, concat_axis=0, tiled=True)


def per_device(right_side, prior_diag, inv_factor, coupling_panel, coupling_owner, coupling_block):
    device_count = lax.axis_size(("arc", "vec"))
    my_index = lax.axis_index(("arc", "vec"))
    arcs_here = coupling_panel.shape[0]
    links = coupling_owner.shape[1]
    blocks_here = right_side.shape[0]
    block_rows = right_side.shape[1]
    rhs_count = right_side.shape[2]
    entries = arcs_here * links
    slot_count = (entries + device_count - 1) // device_count + 1
    owner_all = coupling_owner.reshape(device_count, entries)
    block_all = coupling_block.reshape(device_count, entries)
    position = jnp.arange(entries, dtype=jnp.int32)
    earlier = (owner_all[:, :, None] == owner_all[:, None, :]) & (
        position[None, None, :] < position[None, :, None]
    )
    rank_all = jnp.sum(earlier.astype(jnp.int32), axis=2)
    owner_mine = lax.dynamic_index_in_dim(owner_all, my_index, 0, keepdims=False)
    rank_mine = lax.dynamic_index_in_dim(rank_all, my_index, 0, keepdims=False)
    slot_mine = owner_mine * slot_count + rank_mine
    slot_ids = jnp.arange(slot_count, dtype=jnp.int32)
    matches = (owner_all[:, None, :] == my_index) & (
        rank_all[:, None, :] == slot_ids[None, :, None]
    )
    filled = jnp.any(matches, axis=2).reshape(-1)
    source_block = jnp.sum(jnp.where(matches, block_all[:, None, :], 0), axis=2).reshape(-1)
    block_ids = jnp.arange(blocks_here, dtype=jnp.int32)
    selector = ((source_block[:, None] == block_ids[None, :]) & filled[:, None]).astype(
        jnp.bfloat16
    )
    solution_field = jnp.zeros_like(right_side)
    residual = right_side
    direction = right_side
    res_gram = lax.psum(inner_gram(residual, residual), ("arc", "vec"))
    for sweep_index in range(ITERS):
        local_rounded = direction.astype(jnp.bfloat16)
        outgoing = jnp.where(
            filled[:, None, None], local_rounded[source_block], jnp.zeros((), jnp.bfloat16)
        )
        arrived = trade_out(outgoing)
        fetched = arrived[slot_mine].reshape(arcs_here, links * block_rows, rhs_count)
        coupled = jnp.einsum(
            "apk,akc->apc", coupling_panel, fetched, preferred_element_type=jnp.float32
        ).astype(jnp.bfloat16)
        whitened = jnp.einsum(
            "apq,aqc->apc", inv_factor, coupled, preferred_element_type=jnp.float32
        ).astype(jnp.bfloat16)
        smoothed = jnp.einsum(
            "aqp,aqc->apc", inv_factor, whitened, preferred_element_type=jnp.float32
        ).astype(jnp.bfloat16)
        projected = jnp.einsum(
            "apk,apc->akc", coupling_panel, smoothed, preferred_element_type=jnp.float32
        ).astype(jnp.bfloat16)
        projected = projected.reshape(entries, block_rows, rhs_count)
        returning = (
            jnp.zeros((device_count * slot_count, block_rows, rhs_count), jnp.bfloat16)
            .at[slot_mine]
            .set(projected)
        )
        came_back = trade_back(returning)
        summed = jnp.einsum("sb,src->brc", selector, came_back, preferred_element_type=jnp.float32)
        image_vec = prior_diag[:, :, None] * direction + summed
        curv_gram = lax.psum(inner_gram(direction, image_vec), ("arc", "vec"))
        factor_low = jnp.linalg.cholesky(curv_gram)
        step_mat = jax.scipy.linalg.cho_solve((factor_low, True), res_gram)
        solution_field = solution_field + combine_cols(direction, step_mat)
        residual = residual - combine_cols(image_vec, step_mat)
        if sweep_index + 1 < ITERS:
            new_gram = lax.psum(inner_gram(residual, residual), ("arc", "vec"))
            beta_mat = jax.scipy.linalg.cho_solve((jnp.linalg.cholesky(res_gram), True), new_gram)
            direction = residual + combine_cols(direction, beta_mat)
            res_gram = new_gram
    return (solution_field, residual)


def solution(mesh):
    in_specs = (
        P(("arc", "vec"), None, None),
        P(("arc", "vec"), None),
        P(("arc", "vec"), None, None),
        P(("arc", "vec"), None, None),
        P(),
        P(),
    )
    out_specs = (P(("arc", "vec"), None, None), P(("arc", "vec"), None, None))
    return jax.shard_map(
        per_device, mesh=mesh, in_specs=in_specs, out_specs=out_specs, check_vma=False
    )
```

profile of v0, /device:TPU:1, one launch (start us, length us, event | category | flops | bytes accessed | tf_op | source)
XLA Modules:
  0.0 1106.0 jit_solution(6747091864298645977)
XLA Ops:
  17.7 8.4 gather_fusion
  26.1 7.2 broadcast_select_fusion.1
  33.3 12.4 %all-to-all-start = ((bf16[256,128,128]{2,1,0:T(8,128)(2,1)}), bf16[256,128,128]{2,1,0:T(8,128)(2,1)}, u32[]{:S(2)}, u32[]{:S(2)}) async-start(bf16[256,128,128]{2,1,0:T(8,128)(2,1)} %broadcast_select_fusion.1), calls=%async_computation | async-start | bytes 16777216 | tf_op jit(solution)/shard_map/all_to_all | solution.py:18
  45.8 106.4 %all-to-all-done = bf16[256,128,128]{2,1,0:T(8,128)(2,1)} async-done(((bf16[256,128,128]{2,1,0:T(8,128)(2,1)}), bf16[256,128,128]{2,1,0:T(8,128)(2,1)}, u32[]{:S(2)}, u32[]{:S(2)}) %all-to-all-start) | async-done | bytes 8388640 | tf_op jit(solution)/shard_map/all_to_all | solution.py:18
  158.6 8.2 convolution_convert_fusion.4
  185.4 19.4 %scatter_fusion = bf16[256,128,128]{2,1,0:T(8,128)(2,1)} fusion(bf16[256,128,128]{2,1,0:T(8,128)(2,1)} %broadcast.116.clone, s32[128]{0:T(128)S(1)} %fusion.34, bf16[128,128,128]{2,1,0:T(8,128)(2,1)} %bitcast.106), kind=kCustom, calls=%fused_computation.4 | custom fusion | bytes 12583424 | tf_op jit(solution)/shard_map/scatter | solution.py:82
  213.3 104.7 %all-to-all-done.1 = bf16[256,128,128]{2,1,0:T(8,128)(2,1)} async-done(((bf16[256,128,128]{2,1,0:T(8,128)(2,1)}), bf16[256,128,128]{2,1,0:T(8,128)(2,1)}, u32[]{:S(2)}, u32[]{:S(2)}) %all-to-all-start.1) | async-done | bytes 8388640 | tf_op jit(solution)/shard_map/all_to_all | solution.py:22
  318.0 7.8 fusion.2
  327.6 139.7 %all-reduce.9.cloned.1.call-done = (f32[128,128]{0,1:T(8,128)}, f32[128,128]{0,1:T(8,128)}) async-done(((f32[128,128]{0,1:T(8,128)}, f32[128,128]{0,1:T(8,128)}), (f32[128,128]{0,1:T(8,128)}, f32[128,128]{0,1:T(8,128)})) %all-reduce.9.cloned.1.call-update) | async-done | bytes 131088 | tf_op jit(solution)/shard_map/psum | solution.py:58
  470.1 11.7 %cholesky.70 = f32[128,128]{1,0:T(8,128)S(1)} custom-call(f32[128,128]{1,0:T(8,128)S(1)} %get-tuple-element.18), custom_call_target="Cholesky" | custom-call | tf_op jit(solution)/shard_map/jit(cholesky)/cholesky | solution.py:94
  482.5 11.7 %cholesky.59 = f32[128,128]{1,0:T(8,128)S(1)} custom-call(f32[128,128]{1,0:T(8,128)S(1)} %get-tuple-element.19), custom_call_target="Cholesky" | custom-call | tf_op jit(solution)/shard_map/jit(cholesky)/cholesky | solution.py:88
  495.5 9.8 custom-call.9
  508.5 10.2 all-reduce.7.cloned.1.call-start
  520.2 9.8 custom-call.10
  530.0 114.3 %all-reduce.5.cloned.1.call-done = f32[128,128]{1,0:T(8,128)} async-done(((f32[128,128]{1,0:T(8,128)}), f32[128,128]{1,0:T(8,128)}) %all-reduce.5.cloned.1.call-update) | async-done | bytes 65552 | tf_op jit(solution)/shard_map/psum | solution.py:93
  646.2 8.4 gather_fusion.2
  654.6 7.2 broadcast_select_fusion
  661.8 103.6 %all_to_all.20 = bf16[256,128,128]{2,1,0:T(8,128)(2,1)} all-to-all(bf16[256,128,128]{2,1,0:T(8,128)(2,1)} %broadcast_select_fusion), channel_id=1, replica_groups=mesh['arc'=16,'vec'=8] {'arc','vec'}, dimensions={0} | all-to-all | bytes 16777216 | tf_op jit(solution)/shard_map/all_to_all | solution.py:18
  771.9 9.2 convolution_convert_fusion.1
  800.1 19.4 %scatter_fusion.1 = bf16[256,128,128]{2,1,0:T(8,128)(2,1)} fusion(bf16[256,128,128]{2,1,0:T(8,128)(2,1)} %broadcast.116, s32[128]{0:T(128)S(1)} %fusion.34, bf16[128,128,128]{2,1,0:T(8,128)(2,1)} %bitcast.105), kind=kCustom, calls=%fused_computation.5 | custom fusion | bytes 12583424 | tf_op jit(solution)/shard_map/scatter | solution.py:82
  819.4 106.0 %all_to_all.21 = bf16[256,128,128]{2,1,0:T(8,128)(2,1)S(1)} all-to-all(bf16[256,128,128]{2,1,0:T(8,128)(2,1)} %scatter_fusion.1), channel_id=1, replica_groups=mesh['arc'=16,'vec'=8] {'arc','vec'}, dimensions={0} | all-to-all | bytes 16777216 | tf_op jit(solution)/shard_map/all_to_all | solution.py:22
  933.4 136.1 %all-reduce.7.cloned.1.call-done = f32[128,128]{0,1:T(8,128)} async-done(((f32[128,128]{0,1:T(8,128)}), f32[128,128]{0,1:T(8,128)}) %all-reduce.7.cloned.1.call-update) | async-done | bytes 65552 | tf_op jit(solution)/shard_map/psum | solution.py:87
  1071.2 11.7 %cholesky.81 = f32[128,128]{1,0:T(8,128)S(1)} custom-call(f32[128,128]{1,0:T(8,128)S(1)} %fusion.17), custom_call_target="Cholesky" | custom-call | tf_op jit(solution)/shard_map/jit(cholesky)/cholesky | solution.py:88
  1084.3 9.8 custom-call.11
  (76 shorter events, 98.5 us)
Async XLA Ops:
  7.2 151.4 %copy-start = (bf16[16,256,256]{2,1,0:T(8,128)(2,1)S(1)}, bf16[16,256,256]{2,1,0:T(8,128)(2,1)}, u32[]{:S(2)}) copy-start(bf16[16,256,256]{2,1,0:T(8,128)(2,1)} %param.11) | copy-start | bytes 6291460
  33.3 118.8 %all-to-all-start = ((bf16[256,128,128]{2,1,0:T(8,128)(2,1)}), bf16[256,128,128]{2,1,0:T(8,128)(2,1)}, u32[]{:S(2)}, u32[]{:S(2)}) async-start(bf16[256,128,128]{2,1,0:T(8,128)(2,1)} %broadcast_select_fusion.1), calls=%async_computation | async-start | bytes 16777216 | tf_op jit(solution)/shard_map/all_to_all | solution.py:18
  204.8 7.1 copy-start.1
  204.8 113.2 %all-to-all-start.1 = ((bf16[256,128,128]{2,1,0:T(8,128)(2,1)}), bf16[256,128,128]{2,1,0:T(8,128)(2,1)}, u32[]{:S(2)}, u32[]{:S(2)}) async-start(bf16[256,128,128]{2,1,0:T(8,128)(2,1)} %scatter_fusion), calls=%async_computation.1 | async-start | bytes 16777216 | tf_op jit(solution)/shard_map/all_to_all | solution.py:22
  211.5 114.3 %copy-start.5 = (f32[5,128]{1,0:T(8,128)S(1)}, f32[5,128]{1,0:T(8,128)}, u32[]{:S(2)}) copy-start(f32[5,128]{1,0:T(8,128)} %param.10) | copy-start | bytes 7684
  211.5 255.8 %all-reduce.9.cloned.1.call-start = ((), (), s32[]{:S(2)}) async-start(), calls=%async_computation.6 | async-start | bytes 262144 | tf_op jit(solution)/shard_map/psum | solution.py:58
  327.3 317.1 %all-reduce.5.cloned.1.call-start = ((), (), s32[]{:S(2)}) async-start(), calls=%async_computation.4 | async-start | bytes 131072 | tf_op jit(solution)/shard_map/psum | solution.py:93
  481.8 13.1 %copy-start.4 = (f32[128,128]{1,0:T(8,128)}, f32[128,128]{1,0:T(8,128)S(1)}, u32[]{:S(2)}) copy-start(f32[128,128]{1,0:T(8,128)S(1)} %cholesky.70) | copy-start | bytes 196612
  508.5 560.9 %all-reduce.7.cloned.1.call-start = ((), (), s32[]{:S(2)}) async-start(), calls=%async_computation.5 | async-start | bytes 131072 | tf_op jit(solution)/shard_map/psum | solution.py:87
  925.4 168.7 %copy-start.3 = (f32[128,128]{1,0:T(8,128)S(1)}, f32[128,128]{1,0:T(8,128)}, u32[]{:S(2)}) copy-start(f32[128,128]{1,0:T(8,128)} %all-reduce.5.cloned.1.call-done) | copy-start | bytes 196612
  929.9 0.8 copy-start.2
Sparse Core Ops, SparseCore 0:
  327.4 139.8 all-reduce.8
  508.7 135.6 all-reduce.4
  932.3 137.1 all-reduce.6
where the time goes:
time: 1110 us
  waiting for transfers between devices  601 us (54%)
  blocking collectives  210 us (19%)
  local copies, waits for them, and re-layouts  100 us (9%)
  other arithmetic  92 us (8%)
  matrix products  58.4 us (5%)
  starting transfers between devices  30 us (3%)
  between operations  14.3 us (1%)
    psum x1, waiting for transfers between devices, per_device(): res_gram = lax.psum(inner_gram(residual, residual), ('arc', 'vec'))  140 us
    psum x1, waiting for transfers between devices, per_device(): curv_gram = lax.psum(inner_gram(direction, image_vec), ('arc', 'vec'))  136 us
    psum x1, waiting for transfers between devices, per_device(): new_gram = lax.psum(inner_gram(residual, residual), ('arc', 'vec'))  114 us
    all_to_all x1, waiting for transfers between devices, trade_out(): lax.all_to_all(buffer, ('arc', 'vec'), split_axis=0, concat_axis=0, tiled...  106 us
    all_to_all x1, blocking collectives, trade_back(): lax.all_to_all(buffer, ('arc', 'vec'), split_axis=0, concat_axis=0, tiled...  106 us
    all_to_all x1, waiting for transfers between devices, trade_back(): lax.all_to_all(buffer, ('arc', 'vec'), split_axis=0, concat_axis=0, tiled...  105 us
    all_to_all x1, blocking collectives, trade_out(): lax.all_to_all(buffer, ('arc', 'vec'), split_axis=0, concat_axis=0, tiled...  104 us
    scatter x2, local copies, waits for them, and re-layouts, per_device(): returning = jnp.zeros((device_count * slot_count, block_rows, rhs_count),...  38.7 us
  transfers between devices with their start and end apart: 5, of which 5 were waited for; matrix products, arithmetic and copies ran while one was open for 1% of the time, Pallas kernels for 0%

commit v1 on v0

v1 whole, which is shorter than its diff:
```python
import functools
import jax
import jax.numpy as jnp
from jax import lax
from jax.experimental import pallas as pl
from jax.experimental.pallas import tpu as pltpu
from jax.sharding import PartitionSpec as P
MESH = pl.DeviceIdType.MESH
DIMS = ((0, 1, 2), (1, 2, 0), (2, 0, 1))
CUT = ((0, 112, 208), (208, 320, 432), (432, 528, 640))
OFFS = (0, 3, 1, 2)

def coords():
    arc, vec = lax.axis_index("arc"), lax.axis_index("vec")
    return (arc // 4, arc % 4, vec // 2), vec % 2

def dev(pos, core):
    return (pos[0] * 4 + pos[1], pos[2] * 2 + core)

def moved(pos, dim, off):
    return tuple((p + off) % 4 if d == dim else p for d, p in enumerate(pos))

def entry_barrier(pos, core):
    barrier = pltpu.get_barrier_semaphore()
    for dim in range(3):
        for off in (1, 3):
            pl.semaphore_signal(barrier, inc=1, device_id=dev(moved(pos, dim, off), core), device_id_type=MESH)
    pl.semaphore_signal(barrier, inc=1, device_id=dev(pos, 1 - core), device_id_type=MESH)
    pl.semaphore_wait(barrier, 7)

def gather_all(G, send, recv, csend, crecv, pos, core):
    pend = []
    cpend = []
    nsem = [0]
    ncs = [0]
    def at(sel, cc, rows):
        return G.at[sel[0], sel[1], sel[2], cc, pl.ds(rows[0], rows[1] - rows[0])]
    def make(sel_src, dim, off, rows):
        i = nsem[0]; nsem[0] += 1
        ref = at(sel_src, core, rows)
        return pltpu.make_async_remote_copy(ref, ref, send.at[i], recv.at[i],
            device_id=dev(moved(pos, dim, off), core), device_id_type=MESH)
    def start(sel, dim, off, rows):
        c = make(sel, dim, off, rows); c.start(); pend.append(c); return c
    def cross(sel, rows):
        i = ncs[0]; ncs[0] += 1
        ref = at(sel, core, rows)
        c = pltpu.make_async_remote_copy(ref, ref, csend.at[i], crecv.at[i],
            device_id=dev(pos, 1 - core), device_id_type=MESH)
        c.start(); cpend.append(c)
    def rel(dim, off):
        return moved(pos, dim, off)
    def allof(sel, *dims):
        return tuple(slice(None) if d in dims else s for d, s in enumerate(sel))
    A = [(c[0], c[1]) for c in CUT]; B = [(c[1], c[2]) for c in CUT]; F = [(c[0], c[2]) for c in CUT]
    s1 = {}; f1 = {}; s2 = {}; f2 = {}; s3 = {}; f3 = {}
    def S2(p, o1):
        d1, d2, d3 = DIMS[p]
        for off in (1, 3):
            s2[p, o1, off] = start(moved(pos, d1, o1), d2, off, F[p])
    def S3(p, o2):
        d1, d2, d3 = DIMS[p]
        for off in (1, 3):
            s3[p, o2, off] = start(allof(moved(pos, d2, o2), d1), d3, off, F[p])
    for p in range(3):
        d1 = DIMS[p][0]
        for off in (1, 3):
            s1[p, off] = start(pos, d1, off, F[p])
    for p in range(3):
        S2(p, 0)
    cross(pos, (0, 640))
    for p in range(3):
        d1 = DIMS[p][0]
        s1[p, 1].wait_recv()
        f1[p, 1] = start(rel(d1, 3), d1, 1, A[p])
        s1[p, 3].wait_recv()
        f1[p, 3] = start(rel(d1, 1), d1, 3, B[p])
    for p in range(3):
        S2(p, 3); S2(p, 1)
        d1 = DIMS[p][0]
        cross(rel(d1, 3), F[p]); cross(rel(d1, 1), F[p])
    for p in range(3):
        f1[p, 1].wait_recv(); f1[p, 3].wait_recv()
        S2(p, 2)
        S3(p, 0)
        cross(rel(DIMS[p][0], 2), F[p])
    for o1 in OFFS:
        for p in range(3):
            d1, d2, d3 = DIMS[p]
            s2[p, o1, 1].wait_recv()
            f2[p, o1, 1] = start(moved(rel(d1, o1), d2, 3), d2, 1, A[p])
            s2[p, o1, 3].wait_recv()
            f2[p, o1, 3] = start(moved(rel(d1, o1), d2, 1), d2, 3, B[p])
    for p in range(3):
        d1, d2, d3 = DIMS[p]
        S3(p, 3); S3(p, 1)
        cross(allof(rel(d2, 3), d1), F[p]); cross(allof(rel(d2, 1), d1), F[p])
    for p in range(3):
        d1, d2, d3 = DIMS[p]
        for o1 in OFFS:
            f2[p, o1, 1].wait_recv(); f2[p, o1, 3].wait_recv()
        S3(p, 2)
        cross(allof(rel(d2, 2), d1), F[p])
    for o2 in OFFS:
        for p in range(3):
            d1, d2, d3 = DIMS[p]
            s3[p, o2, 1].wait_recv()
            sel = allof(moved(rel(d2, o2), d3, 3), d1)
            f3[p, o2, 1] = start(sel, d3, 1, A[p])
            cross(sel, F[p])
            s3[p, o2, 3].wait_recv()
            sel = allof(moved(rel(d2, o2), d3, 1), d1)
            f3[p, o2, 3] = start(sel, d3, 3, B[p])
            cross(sel, F[p])
    for o2 in OFFS:
        for p in range(3):
            d1, d2, d3 = DIMS[p]
            f3[p, o2, 1].wait_recv(); f3[p, o2, 3].wait_recv()
            cross(allof(moved(rel(d2, o2), d3, 2), d1), F[p])
    for c in cpend:
        c.wait_recv()
    for c in pend + cpend:
        c.wait_send()
    return nsem[0], ncs[0]

NS, NC = 108, 55


ORDER = (2, 1, 3, 0)
F32, BF16 = jnp.float32, jnp.bfloat16
FULL = [(c[0], c[2]) for c in CUT]; HA = [(c[0], c[1]) for c in CUT]; HB = [(c[1], c[2]) for c in CUT]

def barrier_all(pos, core, far):
    barrier = pltpu.get_barrier_semaphore()
    offs = (1, 2, 3) if far else (1, 3)
    for dim in range(3):
        for off in offs:
            pl.semaphore_signal(barrier, inc=1, device_id=dev(moved(pos, dim, off), core), device_id_type=MESH)
    pl.semaphore_signal(barrier, inc=1, device_id=dev(pos, 1 - core), device_id_type=MESH)
    pl.semaphore_wait(barrier, 3 * len(offs) + 1)

def pieces(p):
    lo, hi = FULL[p]
    out = []
    for b in range(5):
        r0, r1 = max(lo, b * 128), min(hi, b * 128 + 128)
        if r0 < r1:
            out.append((b, r0 - b * 128, r1 - b * 128))
    return out

def rows(r):
    return pl.ds(r[0], r[1] - r[0])

def reduce_scatter(proj, tab, H, W, FR, SR, send, recv, pos, core):
    count = [0]
    pend = []
    tags = {}
    def ring_dim(p, lvl):
        return DIMS[p][2 - lvl]
    def hsel(p, lvl, grp, off):
        d1, d2, d3 = DIMS[p]
        sel = list(pos)
        if lvl == 0:
            sel[d1] = slice(None); sel[d2] = (pos[d2] + grp) % 4; sel[d3] = (pos[d3] + off) % 4
        elif lvl == 1:
            sel[d1] = (pos[d1] + grp) % 4; sel[d2] = (pos[d2] + off) % 4
        else:
            sel[d1] = (pos[d1] + off) % 4
        return tuple(sel)
    def rsel(p, lvl, grp):
        d1, d2, d3 = DIMS[p]
        if lvl == 0:
            return tuple(slice(None) if d == d1 else (pos[d2] + grp) % 4 for d in sorted((d1, d2)))
        if lvl == 1:
            return ((pos[d1] + grp) % 4,)
        return ()
    def wsel(p, lvl, grp, off):
        h = hsel(p, lvl, grp, off)
        return tuple(h[d] for d in sorted(DIMS[p][:2]))
    def source(p, lvl, grp, off, rr):
        if lvl == 0:
            return H.at[(*hsel(p, lvl, grp, off), rows(rr))]
        return W.at[(*wsel(p, lvl, grp, off), rows(rr))]
    def start(src, dst, p, lvl, off, tag):
        i = count[0]; count[0] += 1
        c = pltpu.make_async_remote_copy(src, dst, send.at[i], recv.at[i],
            device_id=dev(moved(pos, ring_dim(p, lvl), off), core), device_id_type=MESH)
        c.start(); pend.append(c); tags[tag] = c
    def send_f(p, lvl, grp):
        r = rsel(p, lvl, grp)
        start(source(p, lvl, grp, 2, HA[p]), FR[lvl].at[(*r, rows(HA[p]))], p, lvl, 1, ("f", p, lvl, grp, 1))
        start(source(p, lvl, grp, 2, HB[p]), FR[lvl].at[(*r, rows(HB[p]))], p, lvl, 3, ("f", p, lvl, grp, 3))
    def send_s(p, lvl, grp, off, half):
        r = rsel(p, lvl, grp)
        rr = (HA if half == 0 else HB)[p]
        start(source(p, lvl, grp, off, rr), SR[lvl].at[(0 if off == 1 else 1, *r, rows(rr))], p, lvl, off, ("s", p, lvl, grp, off, half))
    def chunks(h, r, body):
        if any(isinstance(s, slice) for s in h):
            def step(i, _):
                body(tuple(i if isinstance(s, slice) else s for s in h), tuple(i if isinstance(s, slice) else s for s in r))
                return 0
            lax.fori_loop(0, 4, step, 0)
        else:
            body(h, r)
    def fill(p, grp, off):
        def body(h, r):
            g0 = ((h[0] * 4 + h[1]) * 8 + h[2] * 2 + core) * 5
            for b, r0, r1 in pieces(p):
                rr = pl.ds(r0, r1 - r0)
                e = [tab[(g0 + b) * 4 + k] for k in range(4)]
                v = (proj[e[0], rr] + proj[e[1], rr]) + (proj[e[2], rr] + proj[e[3], rr])
                H[(*h, pl.ds(b * 128 + r0, r1 - r0))] = v
        h = hsel(p, 0, grp, off)
        chunks(h, h, body)
    def add_f(p, lvl, grp, off):
        rr = rows((HA if off == 1 else HB)[p])
        def body(h, r):
            if lvl == 0:
                H[(*h, rr)] = (H[(*h, rr)].astype(F32) + FR[0][(*r, rr)].astype(F32)).astype(BF16)
            else:
                W[(*h, rr)] = W[(*h, rr)] + FR[lvl][(*r, rr)].astype(F32)
        chunks((wsel if lvl else hsel)(p, lvl, grp, off), rsel(p, lvl, grp), body)
    def add_s(p, lvl, grp):
        rr = rows(FULL[p])
        def body(h, r):
            w = r if lvl == 0 else h
            own = H[(*h, rr)].astype(F32) if lvl == 0 else W[(*h, rr)]
            W[(*w, rr)] = own + SR[lvl][(0, *r, rr)].astype(F32) + SR[lvl][(1, *r, rr)].astype(F32)
        chunks((wsel if lvl else hsel)(p, lvl, grp, 0), rsel(p, lvl, grp), body)
    def middle(lvl, groups):
        for grp in groups:
            for p in range(3):
                tags["f", p, lvl, grp, 1].wait_recv()
                add_f(p, lvl, grp, 1)
                send_s(p, lvl, grp, 1, 0)
                tags["f", p, lvl, grp, 3].wait_recv()
                add_f(p, lvl, grp, 3)
                send_s(p, lvl, grp, 3, 1)
    def wait_s(p, lvl, grp):
        for off in (1, 3):
            for half in (0, 1):
                tags["s", p, lvl, grp, off, half].wait_recv()
    for grp in ORDER:
        for p in range(3):
            fill(p, grp, 2)
            send_f(p, 0, grp)
    for grp in ORDER:
        for p in range(3):
            fill(p, grp, 1)
            send_s(p, 0, grp, 1, 1)
            fill(p, grp, 3)
            send_s(p, 0, grp, 3, 0)
    middle(0, ORDER[:2])
    for grp in ORDER:
        for p in range(3):
            fill(p, grp, 0)
    middle(0, ORDER[2:])
    for grp in ORDER:
        for p in range(3):
            wait_s(p, 0, grp)
            add_s(p, 0, grp)
            for o1 in ORDER:
                if grp == 2:
                    send_f(p, 1, o1)
                elif grp == 1:
                    send_s(p, 1, o1, 1, 1)
                elif grp == 3:
                    send_s(p, 1, o1, 3, 0)
    middle(1, ORDER)
    for grp in ORDER:
        for p in range(3):
            wait_s(p, 1, grp)
            add_s(p, 1, grp)
            if grp == 2:
                send_f(p, 2, 0)
            elif grp == 1:
                send_s(p, 2, 0, 1, 1)
            elif grp == 3:
                send_s(p, 2, 0, 3, 0)
    middle(2, (0,))
    for p in range(3):
        wait_s(p, 2, 0)
    def finish():
        for c in pend:
            c.wait_send()
    assert count[0] == NR, count[0]
    def total(r0, r1):
        out = []
        for p in range(3):
            lo, hi = max(r0, FULL[p][0]), min(r1, FULL[p][1])
            if lo < hi:
                rr = pl.ds(lo, hi - lo)
                out.append(W[(*(pos[d] for d in sorted(DIMS[p][:2])), rr)] + SR[2][0, rr].astype(F32) + SR[2][1, rr].astype(F32))
        return jnp.concatenate(out, axis=0)
    return total, finish

NR = 162
def RS_SCRATCH(tb, tc):
    return [pltpu.VMEM((4, 4, 4, 640, 128), BF16), pltpu.VMEM((4, 4, 640, 128), F32),
    pltpu.VMEM((4, 4, 640, 128), BF16), pltpu.VMEM((4, 640, 128), tb), pltpu.VMEM((640, 128), tc),
    pltpu.VMEM((2, 4, 4, 640, 128), BF16), pltpu.VMEM((2, 4, 640, 128), tb), pltpu.VMEM((2, 640, 128), tc),
    pltpu.SemaphoreType.DMA((NR,)), pltpu.SemaphoreType.DMA((NR,))]

def parts_of(half):
    a = -(-half // 24) * 8
    return ((0, a), (a, 2 * a), (2 * a, half))

def all_reduce(M, T, RB, send, recv, pos, core):
    R = M.shape[0]; half = R // 2
    pend = []
    other = dev(pos, 1 - core)
    n = [0]
    def copy(src, dst, to):
        i = n[0]; n[0] += 1
        c = pltpu.make_async_remote_copy(src, dst, send.at[i], recv.at[i], device_id=to, device_id_type=MESH)
        c.start(); pend.append(c); return c
    mine = pl.ds(pl.multiple_of(core * half, 8), half)
    theirs = pl.ds(pl.multiple_of((1 - core) * half, 8), half)
    first = copy(M.at[theirs], T.at[4], other)
    first.wait_recv()
    T[0] = M[mine] + T[4]
    P = parts_of(half)
    got = {}
    def sends(p, k):
        d = DIMS[p][k]
        me = pos[d]
        rr = rows(P[p])
        RB[k, me, rr] = T[k, rr]
        for off in (2, 1, 3):
            got[p, k, off] = copy(T.at[k, rr], RB.at[k, me, rr], dev(moved(pos, d, off), core))
    for p in range(3):
        sends(p, 0)
    for k in range(3):
        for p in range(3):
            rr = rows(P[p])
            for off in (1, 3, 2):
                got[p, k, off].wait_recv()
            T[k + 1, rr] = (RB[k, 0, rr] + RB[k, 1, rr]) + (RB[k, 2, rr] + RB[k, 3, rr])
            if k < 2:
                sends(p, k + 1)
    c = copy(T.at[3], T.at[5], other)
    M[mine] = T[3]
    c.wait_recv()
    first.wait_send()
    M[theirs] = T[5]
    for c in pend[1:]:
        c.wait_send()
    assert n[0] == NG

NG = 29
def AR_SCRATCH(R):
    return [pltpu.VMEM((6, R // 2, 128), F32), pltpu.VMEM((3, 4, R // 2, 128), F32),
            pltpu.SemaphoreType.DMA((NG,)), pltpu.SemaphoreType.DMA((NG,))]

def gram(a, b):
    return lax.dot_general(a, b, (((0,), (0,)), ((), ())), precision=lax.Precision.HIGHEST, preferred_element_type=F32)

def rs_kernel(m, proj, tab, d_ref, prior, image, grams, H, W, FA, FB, FC, SA, SB, SC, send, recv, T, RB, gsend, grecv):
    pos, core = coords()
    barrier_all(pos, core, True)
    total, finish = reduce_scatter(proj, tab, H, W, (FA, FB, FC), (SA, SB, SC), send, recv, pos, core)
    for b in range(5):
        rr = pl.ds(b * 128, 128)
        image[rr] = prior[rr] * d_ref[rr] + total(b * 128, b * 128 + 128).T
    grams[pl.ds(0, 128)] = gram(d_ref[...], image[...])
    if m > 1:
        grams[pl.ds(128, 128)] = gram(image[...], image[...])
        grams[pl.ds(256, 128)] = gram(d_ref[...], d_ref[...])
    all_reduce(grams, T, RB, gsend, grecv, pos, core)
    finish()

def rs_call(m, proj, tab, d, prior):
    V = pl.BlockSpec(memory_space=pltpu.VMEM)
    return pl.pallas_call(functools.partial(rs_kernel, m),
        out_shape=(jax.ShapeDtypeStruct((640, 128), F32), jax.ShapeDtypeStruct((128 * m, 128), F32)),
        in_specs=[V, pl.BlockSpec(memory_space=pltpu.SMEM), V, V], out_specs=(V, V),
        scratch_shapes=RS_SCRATCH(F32, F32) + AR_SCRATCH(128 * m),
        compiler_params=pltpu.CompilerParams(collective_id=1 + m, has_side_effects=True, vmem_limit_bytes=40 << 20),
    )(proj, tab, d, prior)

F32, BF16 = jnp.float32, jnp.bfloat16
def nt(a, b):
    return lax.dot_general(a, b, (((1,), (1,)), ((), ())), preferred_element_type=F32).astype(BF16)
def nn(a, b):
    return lax.dot_general(a, b, (((1,), (0,)), ((), ())), preferred_element_type=F32).astype(BF16)

def k1_kernel(v_ref, idx_ref, panel_h, fac_h, proj, G, panel, fac, send, recv, csend, crecv, lsem, psend, precv):
    pos, core = coords()
    lp = pltpu.make_async_copy(panel_h, panel, lsem.at[0])
    lf = pltpu.make_async_copy(fac_h, fac, lsem.at[1])
    for b in range(5):
        G[pos[0], pos[1], pos[2], core, pl.ds(b * 128, 128)] = v_ref[pl.ds(b * 128, 128)].T.astype(BF16)
    entry_barrier(pos, core)
    lp.start(); lf.start()
    n = gather_all(G, send, recv, csend, crecv, pos, core)
    assert n == (NS, NC), n
    proj[256] = jnp.zeros((128, 128), BF16)
    lp.wait(); lf.wait()
    copies = lambda a: pltpu.make_async_remote_copy(proj.at[pl.ds(a * 8, 8)], proj.at[pl.ds(128 + a * 8, 8)],
        psend.at[a], precv.at[a], device_id=dev(pos, 1 - core), device_id_type=MESH)
    blocks = G.reshape(640, 128, 128)
    def arc(a, _):
        cat = []
        for k in range(8):
            cat.append(blocks[idx_ref[a * 8 + k]])
        x = jnp.concatenate(cat, axis=1)
        f = fac[a]
        s = nn(nt(nt(x, panel[a]), f), f)
        y = nn(s, panel[a])
        for k in range(8):
            proj[a * 8 + k] = y[:, k * 128:(k + 1) * 128]
        copies(a).start()
        return 0
    lax.fori_loop(0, 16, arc, 0)
    def fin(a, _):
        copies(a).wait()
        return 0
    lax.fori_loop(0, 16, fin, 0)

def k1_call(v, idx, panel, fac):
    V = pl.BlockSpec(memory_space=pltpu.VMEM); A = pl.BlockSpec(memory_space=pl.ANY)
    return pl.pallas_call(k1_kernel,
        out_shape=jax.ShapeDtypeStruct((257, 128, 128), BF16),
        in_specs=[V, pl.BlockSpec(memory_space=pltpu.SMEM), A, A], out_specs=V,
        scratch_shapes=[pltpu.VMEM((4, 4, 4, 2, 640, 128), BF16), pltpu.VMEM((16, 256, 1024), BF16), pltpu.VMEM((16, 256, 256), BF16),
            pltpu.SemaphoreType.DMA((NS,)), pltpu.SemaphoreType.DMA((NS,)),
            pltpu.SemaphoreType.DMA((NC,)), pltpu.SemaphoreType.DMA((NC,)), pltpu.SemaphoreType.DMA((2,)),
            pltpu.SemaphoreType.DMA((16,)), pltpu.SemaphoreType.DMA((16,))],
        compiler_params=pltpu.CompilerParams(collective_id=0, has_side_effects=True, vmem_limit_bytes=45 << 20),
    )(v, idx, panel, fac)

HI = lax.Precision.HIGHEST
def mm(a, b): return jnp.dot(a, b, precision=HI)
def tables(owner, block, me, core):
    g = owner * 5 + block
    mine = lax.dynamic_slice_in_dim(g.reshape(128, 128), me, 1, 0).reshape(128)
    theirs = lax.dynamic_slice_in_dim(g.reshape(128, 128), me + 1 - 2 * core, 1, 0).reshape(128)
    def two(row, base):
        e = jnp.arange(128, dtype=jnp.int32)
        hit = row[None, :] == jnp.arange(640, dtype=jnp.int32)[:, None]
        first = jnp.min(jnp.where(hit, e[None], 999), axis=1)
        last = jnp.max(jnp.where(hit, e[None], -1), axis=1)
        return jnp.where(first < 999, first + base, 256), jnp.where(last > first, last + base, 256)
    t = jnp.stack([*two(mine, 0), *two(theirs, 128)], axis=1).reshape(-1).astype(jnp.int32)
    return mine, t
def solve(a, b):
    return jax.scipy.linalg.cho_solve((jnp.linalg.cholesky(a), True), b)
def per_device(right_side, prior_diag, inv_factor, coupling_panel, owner, block):
    me = lax.axis_index(("arc", "vec"))
    core = me % 2
    idx, tab = tables(owner, block, me, core)
    b = right_side.reshape(640, 128)
    prior = jnp.broadcast_to(prior_diag.reshape(640, 1), (640, 128))
    proj = k1_call(b, idx, coupling_panel, inv_factor)
    image, grams = rs_call(3, proj, tab, b, prior)
    c, g2, g0 = grams[:128], grams[128:256], grams[256:]
    alpha = solve(c, g0)
    ca = mm(c, alpha)
    new = g0 - ca - ca.T + mm(alpha.T, mm(g2, alpha))
    beta = solve(g0, new)
    x = mm(b, alpha)
    r = b - mm(image, alpha)
    d = r + mm(b, beta)
    proj = k1_call(d, idx, coupling_panel, inv_factor)
    image, c = rs_call(1, proj, tab, d, prior)
    alpha = solve(c, new)
    x = x + mm(d, alpha)
    r = r - mm(image, alpha)
    return x.reshape(5, 128, 128), r.reshape(5, 128, 128)
def solution(mesh):
    ins = (P(("arc", "vec"), None, None), P(("arc", "vec"), None), P(("arc", "vec"), None, None), P(("arc", "vec"), None, None), P(), P())
    outs = (P(("arc", "vec"), None, None), P(("arc", "vec"), None, None))
    return jax.shard_map(per_device, mesh=mesh, in_specs=ins, out_specs=outs, check_vma=False)
```

time: 1110 us -> 395 us (0.36)
  waiting for transfers between devices: 601 us -> 0 us
  Pallas kernels: 0 us -> 283 us
  blocking collectives: 210 us -> 0 us
  local copies, waits for them, and re-layouts: 100 us -> 17.9 us
  matrix products: 58.4 us -> 9.22 us
  starting transfers between devices: 30 us -> 0 us
  other arithmetic: 92 us -> 76.9 us
  between operations: 14.3 us -> 1.23 us
    psum x3 -> x0, waiting for transfers between devices: 390 us -> none  [the longest x1 140 us: per_device(): res_gram = lax.psum(inner_gram(residual, residual), ('arc', 'vec'))]
    pallas_call x0 -> x4, Pallas kernels: none -> 283 us  [the longest x2 143 us: rs_call(): pl.pallas_call(functools.partial(rs_kernel, m), out_shape=(jax.ShapeDtype...]
    all_to_all x2 -> x0, waiting for transfers between devices: 211 us -> none  [the longest x1 106 us: trade_out(): lax.all_to_all(buffer, ('arc', 'vec'), split_axis=0, concat_axis=0, tiled...]
    all_to_all x2 -> x0, blocking collectives: 210 us -> none  [the longest x1 106 us: trade_back(): lax.all_to_all(buffer, ('arc', 'vec'), split_axis=0, concat_axis=0, tiled...]
    dot_general x15 -> x8, matrix products: 55.2 us -> 5.24 us  [mm(): return jnp.dot(a, b, precision=HI)]
    scatter x2 -> x0, local copies, waits for them, and re-layouts: 38.7 us -> none  [per_device(): returning = jnp.zeros((device_count * slot_count, block_rows, rhs_count),...]
    gather x4 -> x0, local copies, waits for them, and re-layouts: 29.6 us -> none  [the longest x2 16.8 us: per_device(): local_rounded[source_block]]
    all_to_all x2 -> x0, starting transfers between devices: 19.1 us -> none  [the longest x1 12.4 us: trade_out(): lax.all_to_all(buffer, ('arc', 'vec'), split_axis=0, concat_axis=0, tiled...]
  transfers between devices with their start and end apart: 5 -> 0, of which waited for: 5 -> 0; matrix products, arithmetic and copies ran while one was open for 1% -> 0% of each run, Pallas kernels for 0% -> 0%
where the time goes in v1:
time: 395 us; the launch traced here: 388 us
  Pallas kernels  283 us (72%)
  other arithmetic  76.9 us (19%)
  local copies, waits for them, and re-layouts  17.9 us (5%)
  matrix products  9.22 us (2%)
    pallas_call x2, Pallas kernels, rs_call(): pl.pallas_call(functools.partial(rs_kernel, m), out_shape=(jax.ShapeDtype...  143 us
    pallas_call x2, Pallas kernels, k1_call(): pl.pallas_call(k1_kernel, out_shape=jax.ShapeDtypeStruct((257, 128, 128),...  140 us
    another operation x15, other arithmetic, solve(): return jax.scipy.linalg.cho_solve((jnp.linalg.cholesky(a), True), b)  74.1 us
    unnamed x20, local copies, waits for them, and re-layouts  10.7 us

profile of v1, /device:TPU:1, one launch (start us, length us, event | category | flops | bytes accessed | tf_op | source)
XLA Modules:
  0.0 388.2 jit_solution(2032936555247670486)
XLA Ops:
  3.3 1.6 copy-done.2
  4.9 1.0 copy-done.4
  5.8 73.1 %shard_map.77.proj = bf16[257,128,128]{2,1,0:T(8,128)(2,1)} custom-call(f32[640,128]{1,0:T(8,128)S(1)} %bitcast.70, s32[128]{0:T(128)S(1)} %get-tuple-element.23.idx_ref, bf16[16,256,1024]{2,1,0:T(8,128)(2,1)} %panel_h.3, bf16[16,256,256]{2,1,0:T(8,128)(2,1)S(1)} %copy-done.2), custom_call_target="tpu_custom_call" | custom-call | tf_op jit(solution)/shard_map/pallas_call | solution.py:422
  79.1 3.4 copy-done.1
  82.5 72.6 %shard_map.78 = (f32[640,128]{1,0:T(8,128)S(1)}, f32[384,128]{1,0:T(8,128)S(1)}) custom-call(bf16[257,128,128]{2,1,0:T(8,128)(2,1)S(1)} %copy-done.1, s32[2560]{0:T(1024)S(1)} %reshape.103.tab, f32[640,128]{1,0:T(8,128)S(1)} %bitcast.71, f32[640,128]{1,0:T(8,128)S(1)} %broadcast_in_dim.64.prior), custom_call_target="tpu_custom_call" | custom-call | tf_op jit(solution)/shard_map/pallas_call | solution.py:374
  156.8 1.6 copy.35
  158.3 1.5 fusion.13
  159.8 12.5 %cholesky.70 = f32[128,128]{1,0:T(8,128)S(1)} custom-call(f32[128,128]{1,0:T(8,128)} %get-tuple-element.18), custom_call_target="Cholesky" | custom-call | tf_op jit(solution)/shard_map/jit(cholesky)/cholesky | solution.py:447
  173.2 1.3 fusion.2
  174.5 11.3 %custom-call.10 = f32[1,128,128]{1,2,0:T(8,128)} custom-call(f32[1,128,128]{2,1,0:T(8,128)} %fusion.2), custom_call_target="InvertDiagBlocksLowerTriangular" | custom-call | tf_op jit(solution)/shard_map/jit(_cho_solve)/triangular_solve | solution.py:447
  185.8 12.7 %cholesky.59 = f32[128,128]{1,0:T(8,128)S(1)} custom-call(f32[128,128]{1,0:T(8,128)} %get-tuple-element.19), custom_call_target="Cholesky" | custom-call | tf_op jit(solution)/shard_map/jit(cholesky)/cholesky | solution.py:447
  199.2 1.3 fusion.1
  200.4 10.6 %custom-call.9 = f32[1,128,128]{1,2,0:T(8,128)S(1)} custom-call(f32[1,128,128]{2,1,0:T(8,128)} %fusion.1), custom_call_target="InvertDiagBlocksLowerTriangular" | custom-call | tf_op jit(solution)/shard_map/jit(_cho_solve)/triangular_solve | solution.py:447
  212.0 1.0 fusion.14
  214.0 1.6 copy.36
  215.8 1.2 convolution_add_fusion.1
  216.9 1.1 fusion.11
  218.1 1.0 fusion.9
  220.7 67.3 %shard_map.79.proj = bf16[257,128,128]{2,1,0:T(8,128)(2,1)} custom-call(f32[640,128]{1,0:T(8,128)S(1)} %fusion.v_ref.d_ref, s32[128]{0:T(128)S(1)} %get-tuple-element.23.idx_ref, bf16[16,256,1024]{2,1,0:T(8,128)(2,1)} %panel_h.3, bf16[16,256,256]{2,1,0:T(8,128)(2,1)S(1)} %copy-done.3), custom_call_target="tpu_custom_call" | custom-call | tf_op jit(solution)/shard_map/pallas_call | solution.py:422
  288.0 3.4 copy-done
  291.4 70.1 %shard_map.80 = (f32[640,128]{1,0:T(8,128)S(1)}, f32[128,128]{1,0:T(8,128)S(1)}) custom-call(bf16[257,128,128]{2,1,0:T(8,128)(2,1)S(1)} %copy-done, s32[2560]{0:T(1024)S(1)} %reshape.103.tab, f32[640,128]{1,0:T(8,128)S(1)} %fusion.v_ref.d_ref, f32[640,128]{1,0:T(8,128)S(1)} %broadcast_in_dim.64.prior), custom_call_target="tpu_custom_call" | custom-call | tf_op jit(solution)/shard_map/pallas_call | solution.py:374
  361.6 11.7 %cholesky.81 = f32[128,128]{1,0:T(8,128)S(1)} custom-call(f32[128,128]{1,0:T(8,128)S(1)} %fusion.8), custom_call_target="Cholesky" | custom-call | tf_op jit(solution)/shard_map/jit(cholesky)/cholesky | solution.py:447
  374.6 9.8 %custom-call.11 = f32[1,128,128]{1,2,0:T(8,128)S(1)} custom-call(f32[1,128,128]{2,1,0:T(8,128)S(1)} %fusion.3), custom_call_target="InvertDiagBlocksLowerTriangular" | custom-call | tf_op jit(solution)/shard_map/jit(_cho_solve)/triangular_solve | solution.py:447
  385.0 1.1 convolution_subtract_fusion
  (51 shorter events, 13.2 us)
Async XLA Ops:
  3.3 1.6 copy-start.2
  4.9 1.0 copy-start.4
  5.8 73.1 %copy-start.9 = (f32[5,128]{1,0:T(8,128)S(1)}, f32[5,128]{1,0:T(8,128)}, u32[]{:S(2)}) copy-start(f32[5,128]{1,0:T(8,128)} %param.10) | copy-start | bytes 7684
  5.8 73.2 %copy-start.5 = (f32[5,128,128]{2,1,0:T(8,128)S(1)}, f32[5,128,128]{2,1,0:T(8,128)}, u32[]{:S(2)}) copy-start(f32[5,128,128]{2,1,0:T(8,128)} %param.9) | copy-start | bytes 983044
  5.8 214.8 %copy-start.3 = (bf16[16,256,256]{2,1,0:T(8,128)(2,1)S(1)}, bf16[16,256,256]{2,1,0:T(8,128)(2,1)}, u32[]{:S(2)}) copy-start(bf16[16,256,256]{2,1,0:T(8,128)(2,1)} %fac_h.3) | copy-start | bytes 6291460
  79.1 3.4 copy-start.1
  211.1 0.6 copy-start.8
  219.5 0.7 copy-start.6
  288.0 3.4 copy-start
  291.4 93.6 %copy-start.7 = (f32[640,128]{1,0:T(8,128)S(1)}, f32[640,128]{1,0:T(8,128)}, u32[]{:S(2)}) copy-start(f32[640,128]{1,0:T(8,128)} %copy-done.6) | copy-start | bytes 983044

commit v2 on v1

--- a/solution.py
+++ b/solution.py
@@ -375,7 +375,7 @@
         out_shape=(jax.ShapeDtypeStruct((640, 128), F32), jax.ShapeDtypeStruct((128 * m, 128), F32)),
         in_specs=[V, pl.BlockSpec(memory_space=pltpu.SMEM), V, V], out_specs=(V, V),
         scratch_shapes=RS_SCRATCH(F32, F32) + AR_SCRATCH(128 * m),
-        compiler_params=pltpu.CompilerParams(collective_id=1 + m, has_side_effects=True, vmem_limit_bytes=40 << 20),
+        compiler_params=pltpu.CompilerParams(collective_id=1 + m, has_side_effects=True, vmem_limit_bytes=34 << 20),
     )(proj, tab, d, prior)
 
 F32, BF16 = jnp.float32, jnp.bfloat16
@@ -418,7 +418,7 @@
     lax.fori_loop(0, 16, fin, 0)
 
 def k1_call(v, idx, panel, fac):
-    V = pl.BlockSpec(memory_space=pltpu.VMEM); A = pl.BlockSpec(memory_space=pl.ANY)
+    V = pl.BlockSpec(memory_space=pltpu.VMEM); A = pl.BlockSpec(memory_space=pltpu.HBM)
     return pl.pallas_call(k1_kernel,
         out_shape=jax.ShapeDtypeStruct((257, 128, 128), BF16),
         in_specs=[V, pl.BlockSpec(memory_space=pltpu.SMEM), A, A], out_specs=V,
@@ -426,11 +426,80 @@
             pltpu.SemaphoreType.DMA((NS,)), pltpu.SemaphoreType.DMA((NS,)),
             pltpu.SemaphoreType.DMA((NC,)), pltpu.SemaphoreType.DMA((NC,)), pltpu.SemaphoreType.DMA((2,)),
             pltpu.SemaphoreType.DMA((16,)), pltpu.SemaphoreType.DMA((16,))],
-        compiler_params=pltpu.CompilerParams(collective_id=0, has_side_effects=True, vmem_limit_bytes=45 << 20),
+        compiler_params=pltpu.CompilerParams(collective_id=0, has_side_effects=True, vmem_limit_bytes=33 << 20),
     )(v, idx, panel, fac)
 
-HI = lax.Precision.HIGHEST
-def mm(a, b): return jnp.dot(a, b, precision=HI)
+F32 = jnp.float32
+def hdot(a, b, ca=1):
+    return lax.dot_general(a, b, (((ca,), (0,)), ((), ())), precision=lax.Precision.HIGHEST, preferred_element_type=F32)
+
+def negated_inverses(mats):
+    lane = lax.broadcasted_iota(jnp.int32, (8, 128), 1)
+    sub = lax.broadcasted_iota(jnp.int32, (8, 128), 0)
+    wide = lax.broadcasted_iota(jnp.int32, (128, 128), 1)
+    def sweep(_, carry):
+        out = []
+        tops = [a[:8] for a in carry]
+        ws = list(tops)
+        for j in range(0, 8, 2):
+            for m in range(len(ws)):
+                w = ws[m]
+                col0 = jnp.broadcast_to(w[:, j:j + 1], (8, 128))
+                col1 = jnp.broadcast_to(w[:, j + 1:j + 2], (8, 128))
+                row0 = jnp.where(lane == j, 1.0, jnp.where(lane == j + 1, 0.0, jnp.broadcast_to(w[j:j + 1, :], (8, 128))))
+                row1 = jnp.where(lane == j + 1, 1.0, jnp.where(lane == j, 0.0, jnp.broadcast_to(w[j + 1:j + 2, :], (8, 128))))
+                a00 = jnp.broadcast_to(col0[j:j + 1, :], (8, 128))
+                a10 = jnp.broadcast_to(col0[j + 1:j + 2, :], (8, 128))
+                a01 = jnp.broadcast_to(col1[j:j + 1, :], (8, 128))
+                a11 = jnp.broadcast_to(col1[j + 1:j + 2, :], (8, 128))
+                inv = 1.0 / (a00 * a11 - a01 * a10)
+                new0 = (a11 * row0 - a01 * row1) * inv
+                new1 = (a00 * row1 - a10 * row0) * inv
+                w = jnp.where((lane == j) | (lane == j + 1), 0.0, w) - col0 * new0 - col1 * new1
+                ws[m] = jnp.where(sub == j, new0, jnp.where(sub == j + 1, new1, w))
+        for a, p, w in zip(carry, tops, ws):
+            m = hdot(jnp.where(lane < 8, 0.0, p), w, 0)
+            rest = jnp.where(wide < 8, m, a - m)
+            first = jnp.where(lane < 8, -w, w)
+            out.append(pltpu.roll(jnp.concatenate([rest[8:], first], axis=0), 120, 1))
+        return tuple(out)
+    return lax.fori_loop(0, 16, sweep, tuple(mats))
+
+def sym(a):
+    return (a + a.T) * 0.5
+
+def first_kernel(grams, b, image, x, r, d, new):
+    c, g2, g0 = grams[pl.ds(0, 128)], grams[pl.ds(128, 128)], grams[pl.ds(256, 128)]
+    ci, gi = negated_inverses((sym(c), sym(g0)))
+    alpha = -hdot(ci, g0)
+    ca = hdot(c, alpha)
+    ng = g0 - ca - ca.T + hdot(alpha, hdot(g2, alpha), 0)
+    beta = -hdot(gi, ng)
+    new[...] = ng
+    bb = b[...]
+    x[...] = hdot(bb, alpha)
+    rr = bb - hdot(image[...], alpha)
+    r[...] = rr
+    d[...] = rr + hdot(bb, beta)
+
+def last_kernel(c, new, x0, r0, d, image, x, r):
+    (ci,) = negated_inverses((sym(c[...]),))
+    alpha = -hdot(ci, new[...])
+    x[...] = x0[...] + hdot(d[...], alpha)
+    r[...] = r0[...] - hdot(image[...], alpha)
+
+def first_call(grams, b, image):
+    big, small = jax.ShapeDtypeStruct((640, 128), F32), jax.ShapeDtypeStruct((128, 128), F32)
+    V = pl.BlockSpec(memory_space=pltpu.VMEM)
+    return pl.pallas_call(first_kernel, out_shape=(big, big, big, small), in_specs=[V] * 3, out_specs=(V,) * 4,
+        compiler_params=pltpu.CompilerParams(vmem_limit_bytes=16 << 20))(grams, b, image)
+
+def last_call(c, new, x0, r0, d, image):
+    big = jax.ShapeDtypeStruct((640, 128), F32)
+    V = pl.BlockSpec(memory_space=pltpu.VMEM)
+    return pl.pallas_call(last_kernel, out_shape=(big, big), in_specs=[V] * 6, out_specs=(V,) * 2,
+        compiler_params=pltpu.CompilerParams(vmem_limit_bytes=16 << 20))(c, new, x0, r0, d, image)
+
 def tables(owner, block, me, core):
     g = owner * 5 + block
     mine = lax.dynamic_slice_in_dim(g.reshape(128, 128), me, 1, 0).reshape(128)
@@ -443,8 +512,6 @@
         return jnp.where(first < 999, first + base, 256), jnp.where(last > first, last + base, 256)
     t = jnp.stack([*two(mine, 0), *two(theirs, 128)], axis=1).reshape(-1).astype(jnp.int32)
     return mine, t
-def solve(a, b):
-    return jax.scipy.linalg.cho_solve((jnp.linalg.cholesky(a), True), b)
 def per_device(right_side, prior_diag, inv_factor, coupling_panel, owner, block):
     me = lax.axis_index(("arc", "vec"))
     core = me % 2
@@ -453,19 +520,10 @@
     prior = jnp.broadcast_to(prior_diag.reshape(640, 1), (640, 128))
     proj = k1_call(b, idx, coupling_panel, inv_factor)
     image, grams = rs_call(3, proj, tab, b, prior)
-    c, g2, g0 = grams[:128], grams[128:256], grams[256:]
-    alpha = solve(c, g0)
-    ca = mm(c, alpha)
-    new = g0 - ca - ca.T + mm(alpha.T, mm(g2, alpha))
-    beta = solve(g0, new)
-    x = mm(b, alpha)
-    r = b - mm(image, alpha)
-    d = r + mm(b, beta)
+    x, r, d, new = first_call(grams, b, image)
     proj = k1_call(d, idx, coupling_panel, inv_factor)
     image, c = rs_call(1, proj, tab, d, prior)
-    alpha = solve(c, new)
-    x = x + mm(d, alpha)
-    r = r - mm(image, alpha)
+    x, r = last_call(c, new, x, r, d, image)
     return x.reshape(5, 128, 128), r.reshape(5, 128, 128)
 def solution(mesh):
     ins = (P(("arc", "vec"), None, None), P(("arc", "vec"), None), P(("arc", "vec"), None, None), P(("arc", "vec"), None, None), P(), P())

time: 395 us -> 317 us (0.80); the launches traced: 388 us -> 317 us
  other arithmetic: 76.9 us -> 1.32 us
  Pallas kernels: 283 us -> 306 us
  local copies, waits for them, and re-layouts: 17.9 us -> 8 us
  matrix products: 9.22 us -> 0 us
    another operation x15 -> x0, other arithmetic: 74.1 us -> none  [solve(): return jax.scipy.linalg.cho_solve((jnp.linalg.cholesky(a), True), b)]
    pallas_call x0 -> x2, Pallas kernels: none -> 28.5 us  [the longest x1 14.7 us: first_call(): pl.pallas_call(first_kernel, out_shape=(big, big, big, small), in_specs=[...]
    dot_general x8 -> x0, matrix products: 5.24 us -> none  [mm(): return jnp.dot(a, b, precision=HI)]
    pallas_call x2, Pallas kernels: 140 us -> 135 us  [k1_call(): pl.pallas_call(k1_kernel, out_shape=jax.ShapeDtypeStruct((257, 128, 128),...]
    unnamed x20 -> x12, local copies, waits for them, and re-layouts: 10.7 us -> 5.95 us
    another operation x6 -> x0, matrix products: 3.98 us -> none  [solve(): return jax.scipy.linalg.cho_solve((jnp.linalg.cholesky(a), True), b)]
where the time goes in v2:
time: 317 us
  Pallas kernels  306 us (97%)
  local copies, waits for them, and re-layouts  8 us (3%)
    pallas_call x2, Pallas kernels, rs_call(): pl.pallas_call(functools.partial(rs_kernel, m), out_shape=(jax.ShapeDtype...  143 us
    pallas_call x2, Pallas kernels, k1_call(): pl.pallas_call(k1_kernel, out_shape=jax.ShapeDtypeStruct((257, 128, 128),...  135 us
    pallas_call x1, Pallas kernels, first_call(): pl.pallas_call(first_kernel, out_shape=(big, big, big, small), in_specs=[...  14.7 us
    pallas_call x1, Pallas kernels, last_call(): pl.pallas_call(last_kernel, out_shape=(big, big), in_specs=[V] * 6, out_s...  13.8 us

profile of v2, /device:TPU:1, one launch (start us, length us, event | category | flops | bytes accessed | tf_op | source)
XLA Modules:
  0.0 316.6 jit_solution(15623973983999954352)
XLA Ops:
  0.6 0.9 multiply_add_fusion
  1.5 0.8 broadcast_in_dim.63.prior
  2.4 0.3 copy.10
  2.7 0.5 reshape.91
  3.2 0.4 select_reduce_fusion.1
  3.7 0.2 copy.11
  3.9 0.2 reshape.93.tab
  4.1 0.0 copy-start
  4.1 3.4 %copy-done = bf16[16,256,1024]{2,1,0:T(8,128)(2,1)S(1)} copy-done((bf16[16,256,1024]{2,1,0:T(8,128)(2,1)S(1)}, bf16[16,256,1024]{2,1,0:T(8,128)(2,1)}, u32[]{:S(2)}) %copy-start) | copy-done | bytes 8388632
  7.5 0.0 copy-start.2
  7.5 1.6 copy-done.2
  9.1 0.0 copy-start.4
  9.1 1.0 copy-done.4
  10.1 0.0 copy-start.5
  10.1 70.4 %shard_map.77.proj = bf16[257,128,128]{2,1,0:T(8,128)(2,1)S(1)} custom-call(f32[640,128]{1,0:T(8,128)S(1)} %bitcast.8, s32[128]{0:T(128)S(1)} %get-tuple-element.27.idx_ref, bf16[16,256,1024]{2,1,0:T(8,128)(2,1)S(1)} %copy-done, bf16[16,256,256]{2,1,0:T(8,128)(2,1)S(1)} %copy-done.2), custom_call_target="tpu_custom_call" | custom-call | tf_op jit(solution)/shard_map/pallas_call | solution.py:422
  80.5 0.0 copy-done.5
  80.5 0.0 copy-start.1
  80.5 72.7 %shard_map.78 = (f32[640,128]{1,0:T(8,128)S(1)}, f32[384,128]{1,0:T(8,128)S(1)}) custom-call(bf16[257,128,128]{2,1,0:T(8,128)(2,1)S(1)} %shard_map.77.proj, s32[2560]{0:T(1024)S(1)} %reshape.93.tab, f32[640,128]{1,0:T(8,128)S(1)} %bitcast.9, f32[640,128]{1,0:T(8,128)S(1)} %broadcast_in_dim.63.prior), custom_call_target="tpu_custom_call" | custom-call | tf_op jit(solution)/shard_map/pallas_call | solution.py:374
  153.2 14.7 %shard_map.79 = (f32[640,128]{1,0:T(8,128)S(1)}, f32[640,128]{1,0:T(8,128)S(1)}, f32[640,128]{1,0:T(8,128)S(1)}, f32[128,128]{1,0:T(8,128)S(1)}) custom-call(f32[384,128]{1,0:T(8,128)S(1)} %get-tuple-element.12.grams, f32[640,128]{1,0:T(8,128)S(1)} %bitcast.10, f32[640,128]{1,0:T(8,128)S(1)} %get-tuple-element.13.image), custom_call_target="tpu_custom_call" | custom-call | tf_op jit(solution)/shard_map/pallas_call | solution.py:494
  167.9 0.0 copy-done.3
  167.9 0.0 copy-done.1
  167.9 64.8 %shard_map.80.proj = bf16[257,128,128]{2,1,0:T(8,128)(2,1)S(1)} custom-call(f32[640,128]{1,0:T(8,128)S(1)} %get-tuple-element.14.v_ref.d_ref.d, s32[128]{0:T(128)S(1)} %get-tuple-element.27.idx_ref, bf16[16,256,1024]{2,1,0:T(8,128)(2,1)S(1)} %copy-done.1, bf16[16,256,256]{2,1,0:T(8,128)(2,1)S(1)} %copy-done.3), custom_call_target="tpu_custom_call" | custom-call | tf_op jit(solution)/shard_map/pallas_call | solution.py:422
  232.7 70.2 %shard_map.81 = (f32[640,128]{1,0:T(8,128)S(1)}, f32[128,128]{1,0:T(8,128)S(1)}) custom-call(bf16[257,128,128]{2,1,0:T(8,128)(2,1)S(1)} %shard_map.80.proj, s32[2560]{0:T(1024)S(1)} %reshape.93.tab, f32[640,128]{1,0:T(8,128)S(1)} %get-tuple-element.14.v_ref.d_ref.d, f32[640,128]{1,0:T(8,128)S(1)} %broadcast_in_dim.63.prior), custom_call_target="tpu_custom_call" | custom-call | tf_op jit(solution)/shard_map/pallas_call | solution.py:374
  302.9 13.8 %shard_map.82 = (f32[640,128]{1,0:T(8,128)}, f32[640,128]{1,0:T(8,128)}) custom-call(f32[128,128]{1,0:T(8,128)S(1)} %get-tuple-element.15.c, f32[128,128]{1,0:T(8,128)S(1)} %get-tuple-element.16.new, f32[640,128]{1,0:T(8,128)S(1)} %get-tuple-element.17.x0, f32[640,128]{1,0:T(8,128)S(1)} %get-tuple-element.18.r0, ...), custom_call_target="tpu_custom_call" | custom-call | tf_op jit(solution)/shard_map/pallas_call | solution.py:500
  (7 shorter events, 0.1 us)
Async XLA Ops:
  4.1 3.4 %copy-start = (bf16[16,256,1024]{2,1,0:T(8,128)(2,1)S(1)}, bf16[16,256,1024]{2,1,0:T(8,128)(2,1)}, u32[]{:S(2)}) copy-start(bf16[16,256,1024]{2,1,0:T(8,128)(2,1)} %panel_h.3) | copy-start | bytes 25165828
  7.5 1.6 copy-start.2
  9.1 1.0 copy-start.4
  10.1 70.4 %copy-start.5 = (f32[5,128,128]{2,1,0:T(8,128)S(1)}, f32[5,128,128]{2,1,0:T(8,128)}, u32[]{:S(2)}) copy-start(f32[5,128,128]{2,1,0:T(8,128)} %param.6) | copy-start | bytes 983044
  10.1 157.8 %copy-start.3 = (bf16[16,256,256]{2,1,0:T(8,128)(2,1)S(1)}, bf16[16,256,256]{2,1,0:T(8,128)(2,1)}, u32[]{:S(2)}) copy-start(bf16[16,256,256]{2,1,0:T(8,128)(2,1)} %fac_h.3) | copy-start | bytes 6291460
  80.5 87.4 %copy-start.1 = (bf16[16,256,1024]{2,1,0:T(8,128)(2,1)S(1)}, bf16[16,256,1024]{2,1,0:T(8,128)(2,1)}, u32[]{:S(2)}) copy-start(bf16[16,256,1024]{2,1,0:T(8,128)(2,1)} %panel_h.3) | copy-start | bytes 25165828

commit v3 on v2

--- a/solution.py
+++ b/solution.py
@@ -151,7 +151,7 @@
 def rows(r):
     return pl.ds(r[0], r[1] - r[0])
 
-def reduce_scatter(proj, tab, H, W, FR, SR, send, recv, pos, core):
+def reduce_scatter(proj, tab, H, W, Q, FR, SR, send, recv, pos, core):
     count = [0]
     pend = []
     tags = {}
@@ -180,7 +180,7 @@
     def source(p, lvl, grp, off, rr):
         if lvl == 0:
             return H.at[(*hsel(p, lvl, grp, off), rows(rr))]
-        return W.at[(*wsel(p, lvl, grp, off), rows(rr))]
+        return (Q if lvl == 1 else W).at[(*wsel(p, lvl, grp, off), rows(rr))]
     def start(src, dst, p, lvl, off, tag):
         i = count[0]; count[0] += 1
         c = pltpu.make_async_remote_copy(src, dst, send.at[i], recv.at[i],
@@ -217,15 +217,20 @@
         def body(h, r):
             if lvl == 0:
                 H[(*h, rr)] = (H[(*h, rr)].astype(F32) + FR[0][(*r, rr)].astype(F32)).astype(BF16)
+            elif lvl == 1:
+                Q[(*h, rr)] = (W[(*h, rr)] + FR[1][(*r, rr)].astype(F32)).astype(BF16)
             else:
-                W[(*h, rr)] = W[(*h, rr)] + FR[lvl][(*r, rr)].astype(F32)
+                W[(*h, rr)] = W[(*h, rr)] + FR[2][(*r, rr)]
         chunks((wsel if lvl else hsel)(p, lvl, grp, off), rsel(p, lvl, grp), body)
     def add_s(p, lvl, grp):
         rr = rows(FULL[p])
         def body(h, r):
             w = r if lvl == 0 else h
             own = H[(*h, rr)].astype(F32) if lvl == 0 else W[(*h, rr)]
-            W[(*w, rr)] = own + SR[lvl][(0, *r, rr)].astype(F32) + SR[lvl][(1, *r, rr)].astype(F32)
+            v = own + SR[lvl][(0, *r, rr)].astype(F32) + SR[lvl][(1, *r, rr)].astype(F32)
+            W[(*w, rr)] = v
+            if lvl == 0 and grp:
+                Q[(*w, rr)] = v.astype(BF16)
         chunks((wsel if lvl else hsel)(p, lvl, grp, 0), rsel(p, lvl, grp), body)
     def middle(lvl, groups):
         for grp in groups:
@@ -296,7 +301,7 @@
 
 NR = 162
 def RS_SCRATCH(tb, tc):
-    return [pltpu.VMEM((4, 4, 4, 640, 128), BF16), pltpu.VMEM((4, 4, 640, 128), F32),
+    return [pltpu.VMEM((4, 4, 4, 640, 128), BF16), pltpu.VMEM((4, 4, 640, 128), F32), pltpu.VMEM((4, 4, 640, 128), BF16),
     pltpu.VMEM((4, 4, 640, 128), BF16), pltpu.VMEM((4, 640, 128), tb), pltpu.VMEM((640, 128), tc),
     pltpu.VMEM((2, 4, 4, 640, 128), BF16), pltpu.VMEM((2, 4, 640, 128), tb), pltpu.VMEM((2, 640, 128), tc),
     pltpu.SemaphoreType.DMA((NR,)), pltpu.SemaphoreType.DMA((NR,))]
@@ -355,10 +360,10 @@
 def gram(a, b):
     return lax.dot_general(a, b, (((0,), (0,)), ((), ())), precision=lax.Precision.HIGHEST, preferred_element_type=F32)
 
-def rs_kernel(m, proj, tab, d_ref, prior, image, grams, H, W, FA, FB, FC, SA, SB, SC, send, recv, T, RB, gsend, grecv):
+def rs_kernel(m, proj, tab, d_ref, prior, image, grams, H, W, Q, FA, FB, FC, SA, SB, SC, send, recv, T, RB, gsend, grecv):
     pos, core = coords()
     barrier_all(pos, core, True)
-    total, finish = reduce_scatter(proj, tab, H, W, (FA, FB, FC), (SA, SB, SC), send, recv, pos, core)
+    total, finish = reduce_scatter(proj, tab, H, W, Q, (FA, FB, FC), (SA, SB, SC), send, recv, pos, core)
     for b in range(5):
         rr = pl.ds(b * 128, 128)
         image[rr] = prior[rr] * d_ref[rr] + total(b * 128, b * 128 + 128).T
@@ -374,11 +379,12 @@
     return pl.pallas_call(functools.partial(rs_kernel, m),
         out_shape=(jax.ShapeDtypeStruct((640, 128), F32), jax.ShapeDtypeStruct((128 * m, 128), F32)),
         in_specs=[V, pl.BlockSpec(memory_space=pltpu.SMEM), V, V], out_specs=(V, V),
-        scratch_shapes=RS_SCRATCH(F32, F32) + AR_SCRATCH(128 * m),
+        scratch_shapes=RS_SCRATCH(BF16, F32) + AR_SCRATCH(128 * m),
         compiler_params=pltpu.CompilerParams(collective_id=1 + m, has_side_effects=True, vmem_limit_bytes=34 << 20),
     )(proj, tab, d, prior)
 
 F32, BF16 = jnp.float32, jnp.bfloat16
+GROUP = 4
 def nt(a, b):
     return lax.dot_general(a, b, (((1,), (1,)), ((), ())), preferred_element_type=F32).astype(BF16)
 def nn(a, b):
@@ -399,19 +405,19 @@
     copies = lambda a: pltpu.make_async_remote_copy(proj.at[pl.ds(a * 8, 8)], proj.at[pl.ds(128 + a * 8, 8)],
         psend.at[a], precv.at[a], device_id=dev(pos, 1 - core), device_id_type=MESH)
     blocks = G.reshape(640, 128, 128)
-    def arc(a, _):
-        cat = []
-        for k in range(8):
-            cat.append(blocks[idx_ref[a * 8 + k]])
-        x = jnp.concatenate(cat, axis=1)
-        f = fac[a]
-        s = nn(nt(nt(x, panel[a]), f), f)
-        y = nn(s, panel[a])
-        for k in range(8):
-            proj[a * 8 + k] = y[:, k * 128:(k + 1) * 128]
-        copies(a).start()
+    def arcs(i, _):
+        mine = [i * GROUP + j for j in range(GROUP)]
+        xs = [jnp.concatenate([blocks[idx_ref[a * 8 + k]] for k in range(8)], axis=1) for a in mine]
+        xs = [nt(x, panel[a]) for x, a in zip(xs, mine)]
+        xs = [nt(x, fac[a]) for x, a in zip(xs, mine)]
+        xs = [nn(x, fac[a]) for x, a in zip(xs, mine)]
+        for x, a in zip(xs, mine):
+            y = nn(x, panel[a])
+            for k in range(8):
+                proj[a * 8 + k] = y[:, k * 128:(k + 1) * 128]
+            copies(a).start()
         return 0
-    lax.fori_loop(0, 16, arc, 0)
+    lax.fori_loop(0, 16 // GROUP, arcs, 0)
     def fin(a, _):
         copies(a).wait()
         return 0
@@ -427,7 +433,7 @@
             pltpu.SemaphoreType.DMA((NC,)), pltpu.SemaphoreType.DMA((NC,)), pltpu.SemaphoreType.DMA((2,)),
             pltpu.SemaphoreType.DMA((16,)), pltpu.SemaphoreType.DMA((16,))],
         compiler_params=pltpu.CompilerParams(collective_id=0, has_side_effects=True, vmem_limit_bytes=33 << 20),
-    )(v, idx, panel, fac)
+    )(v, idx, pltpu.with_memory_space_constraint(panel, pltpu.HBM), pltpu.with_memory_space_constraint(fac, pltpu.HBM))
 
 F32 = jnp.float32
 def hdot(a, b, ca=1):

time: 317 us -> 286 us (0.902)
  Pallas kernels: 306 us -> 281 us
  local copies, waits for them, and re-layouts: 8 us -> 3.02 us
    pallas_call x2, Pallas kernels: 135 us -> 122 us  [k1_call(): pl.pallas_call(k1_kernel, out_shape=jax.ShapeDtypeStruct((257, 128, 128),...]
    pallas_call x2, Pallas kernels: 143 us -> 131 us  [rs_call(): pl.pallas_call(functools.partial(rs_kernel, m), out_shape=(jax.ShapeDtype...]
    unnamed x12 -> x4, local copies, waits for them, and re-layouts: 5.95 us -> 0.97 us
where the time goes in v3:
time: 286 us
  Pallas kernels  281 us (98%)
  local copies, waits for them, and re-layouts  3.02 us (1%)
    pallas_call x2, Pallas kernels, rs_call(): pl.pallas_call(functools.partial(rs_kernel, m), out_shape=(jax.ShapeDtype...  131 us
    pallas_call x2, Pallas kernels, k1_call(): pl.pallas_call(k1_kernel, out_shape=jax.ShapeDtypeStruct((257, 128, 128),...  122 us
    pallas_call x1, Pallas kernels, first_call(): pl.pallas_call(first_kernel, out_shape=(big, big, big, small), in_specs=[...  14.7 us
    pallas_call x1, Pallas kernels, last_call(): pl.pallas_call(last_kernel, out_shape=(big, big), in_specs=[V] * 6, out_s...  13.8 us

profile of v3, /device:TPU:1, one launch (start us, length us, event | category | flops | bytes accessed | tf_op | source)
XLA Modules:
  0.0 286.3 jit_solution(6750717819975275735)
XLA Ops:
  0.6 0.9 multiply_add_fusion
  1.5 0.8 broadcast_in_dim.63.prior
  2.4 0.3 copy.10
  2.7 0.5 reshape.91
  3.2 0.4 select_reduce_fusion.1
  3.7 0.2 copy.11
  3.9 0.2 reshape.93.tab
  4.1 0.0 copy-start
  4.1 1.0 copy-done
  5.1 0.0 copy-start.1
  5.1 63.9 %shard_map.77.proj = bf16[257,128,128]{2,1,0:T(8,128)(2,1)S(1)} custom-call(f32[640,128]{1,0:T(8,128)S(1)} %bitcast.8, s32[128]{0:T(128)S(1)} %get-tuple-element.27.idx_ref, bf16[16,256,1024]{2,1,0:T(8,128)(2,1)} %panel_h.3, bf16[16,256,256]{2,1,0:T(8,128)(2,1)} %fac_h.3), custom_call_target="tpu_custom_call" | custom-call | tf_op jit(solution)/shard_map/pallas_call | solution.py:428
  69.0 0.0 copy-done.1
  69.0 66.5 %shard_map.78 = (f32[640,128]{1,0:T(8,128)S(1)}, f32[384,128]{1,0:T(8,128)S(1)}) custom-call(bf16[257,128,128]{2,1,0:T(8,128)(2,1)S(1)} %shard_map.77.proj, s32[2560]{0:T(1024)S(1)} %reshape.93.tab, f32[640,128]{1,0:T(8,128)S(1)} %bitcast.9, f32[640,128]{1,0:T(8,128)S(1)} %broadcast_in_dim.63.prior), custom_call_target="tpu_custom_call" | custom-call | tf_op jit(solution)/shard_map/pallas_call | solution.py:379
  135.5 14.7 %shard_map.79 = (f32[640,128]{1,0:T(8,128)S(1)}, f32[640,128]{1,0:T(8,128)S(1)}, f32[640,128]{1,0:T(8,128)S(1)}, f32[128,128]{1,0:T(8,128)S(1)}) custom-call(f32[384,128]{1,0:T(8,128)S(1)} %get-tuple-element.12.grams, f32[640,128]{1,0:T(8,128)S(1)} %bitcast.10, f32[640,128]{1,0:T(8,128)S(1)} %get-tuple-element.13.image), custom_call_target="tpu_custom_call" | custom-call | tf_op jit(solution)/shard_map/pallas_call | solution.py:500
  150.2 58.2 %shard_map.80.proj = bf16[257,128,128]{2,1,0:T(8,128)(2,1)S(1)} custom-call(f32[640,128]{1,0:T(8,128)S(1)} %get-tuple-element.14.v_ref.d_ref.d, s32[128]{0:T(128)S(1)} %get-tuple-element.27.idx_ref, bf16[16,256,1024]{2,1,0:T(8,128)(2,1)} %panel_h.3, bf16[16,256,256]{2,1,0:T(8,128)(2,1)} %fac_h.3), custom_call_target="tpu_custom_call" | custom-call | tf_op jit(solution)/shard_map/pallas_call | solution.py:428
  208.4 64.1 %shard_map.81 = (f32[640,128]{1,0:T(8,128)S(1)}, f32[128,128]{1,0:T(8,128)S(1)}) custom-call(bf16[257,128,128]{2,1,0:T(8,128)(2,1)S(1)} %shard_map.80.proj, s32[2560]{0:T(1024)S(1)} %reshape.93.tab, f32[640,128]{1,0:T(8,128)S(1)} %get-tuple-element.14.v_ref.d_ref.d, f32[640,128]{1,0:T(8,128)S(1)} %broadcast_in_dim.63.prior), custom_call_target="tpu_custom_call" | custom-call | tf_op jit(solution)/shard_map/pallas_call | solution.py:379
  272.5 13.8 %shard_map.82 = (f32[640,128]{1,0:T(8,128)}, f32[640,128]{1,0:T(8,128)}) custom-call(f32[128,128]{1,0:T(8,128)S(1)} %get-tuple-element.15.c, f32[128,128]{1,0:T(8,128)S(1)} %get-tuple-element.16.new, f32[640,128]{1,0:T(8,128)S(1)} %get-tuple-element.17.x0, f32[640,128]{1,0:T(8,128)S(1)} %get-tuple-element.18.r0, ...), custom_call_target="tpu_custom_call" | custom-call | tf_op jit(solution)/shard_map/pallas_call | solution.py:506
  (6 shorter events, 0.0 us)
Async XLA Ops:
  4.1 1.0 copy-start
  5.1 63.9 %copy-start.1 = (f32[5,128,128]{2,1,0:T(8,128)S(1)}, f32[5,128,128]{2,1,0:T(8,128)}, u32[]{:S(2)}) copy-start(f32[5,128,128]{2,1,0:T(8,128)} %param.6) | copy-start | bytes 983044

commit v4 on v3

--- a/solution.py
+++ b/solution.py
@@ -26,7 +26,7 @@
         for off in (1, 3):
             pl.semaphore_signal(barrier, inc=1, device_id=dev(moved(pos, dim, off), core), device_id_type=MESH)
     pl.semaphore_signal(barrier, inc=1, device_id=dev(pos, 1 - core), device_id_type=MESH)
-    pl.semaphore_wait(barrier, 7)
+    return lambda: pl.semaphore_wait(barrier, 7)
 
 def gather_all(G, send, recv, csend, crecv, pos, core):
     pend = []
@@ -66,8 +66,14 @@
         d1 = DIMS[p][0]
         for off in (1, 3):
             s1[p, off] = start(pos, d1, off, F[p])
+    def S3one(p, o1):
+        d1, d2, d3 = DIMS[p]
+        for off in (1, 3):
+            s3[p, 0, off, o1] = start(moved(pos, d1, o1), d3, off, F[p])
     for p in range(3):
         S2(p, 0)
+    for p in range(3):
+        S3one(p, 0)
     cross(pos, (0, 640))
     for p in range(3):
         d1 = DIMS[p][0]
@@ -78,11 +84,12 @@
     for p in range(3):
         S2(p, 3); S2(p, 1)
         d1 = DIMS[p][0]
+        S3one(p, 3); S3one(p, 1)
         cross(rel(d1, 3), F[p]); cross(rel(d1, 1), F[p])
     for p in range(3):
         f1[p, 1].wait_recv(); f1[p, 3].wait_recv()
         S2(p, 2)
-        S3(p, 0)
+        S3one(p, 2)
         cross(rel(DIMS[p][0], 2), F[p])
     for o1 in OFFS:
         for p in range(3):
@@ -101,14 +108,17 @@
             f2[p, o1, 1].wait_recv(); f2[p, o1, 3].wait_recv()
         S3(p, 2)
         cross(allof(rel(d2, 2), d1), F[p])
+    def arrived(p, o2, off):
+        for c in ([s3[p, 0, off, o1] for o1 in OFFS] if o2 == 0 else [s3[p, o2, off]]):
+            c.wait_recv()
     for o2 in OFFS:
         for p in range(3):
             d1, d2, d3 = DIMS[p]
-            s3[p, o2, 1].wait_recv()
+            arrived(p, o2, 1)
             sel = allof(moved(rel(d2, o2), d3, 3), d1)
             f3[p, o2, 1] = start(sel, d3, 1, A[p])
             cross(sel, F[p])
-            s3[p, o2, 3].wait_recv()
+            arrived(p, o2, 3)
             sel = allof(moved(rel(d2, o2), d3, 1), d1)
             f3[p, o2, 3] = start(sel, d3, 3, B[p])
             cross(sel, F[p])
@@ -123,21 +133,21 @@
         c.wait_send()
     return nsem[0], ncs[0]
 
-NS, NC = 108, 55
+NS, NC = 126, 55
 
 
 ORDER = (2, 1, 3, 0)
 F32, BF16 = jnp.float32, jnp.bfloat16
 FULL = [(c[0], c[2]) for c in CUT]; HA = [(c[0], c[1]) for c in CUT]; HB = [(c[1], c[2]) for c in CUT]
 
-def barrier_all(pos, core, far):
+def barrier_all(pos, core):
     barrier = pltpu.get_barrier_semaphore()
-    offs = (1, 2, 3) if far else (1, 3)
     for dim in range(3):
-        for off in offs:
-            pl.semaphore_signal(barrier, inc=1, device_id=dev(moved(pos, dim, off), core), device_id_type=MESH)
+        for off in (1, 2, 3):
+            for cc in (0, 1):
+                pl.semaphore_signal(barrier, inc=1, device_id=dev(moved(pos, dim, off), cc), device_id_type=MESH)
     pl.semaphore_signal(barrier, inc=1, device_id=dev(pos, 1 - core), device_id_type=MESH)
-    pl.semaphore_wait(barrier, 3 * len(offs) + 1)
+    return lambda: pl.semaphore_wait(barrier, 19)
 
 def pieces(p):
     lo, hi = FULL[p]
@@ -151,7 +161,7 @@
 def rows(r):
     return pl.ds(r[0], r[1] - r[0])
 
-def reduce_scatter(proj, tab, H, W, Q, FR, SR, send, recv, pos, core):
+def reduce_scatter(proj, tab, H, W, Q, FR, SR, send, recv, pos, core, entered):
     count = [0]
     pend = []
     tags = {}
@@ -248,6 +258,8 @@
     for grp in ORDER:
         for p in range(3):
             fill(p, grp, 2)
+            if grp == ORDER[0] and p == 0:
+                entered()
             send_f(p, 0, grp)
     for grp in ORDER:
         for p in range(3):
@@ -310,68 +322,75 @@
     a = -(-half // 24) * 8
     return ((0, a), (a, 2 * a), (2 * a, half))
 
-def all_reduce(M, T, RB, send, recv, pos, core):
-    R = M.shape[0]; half = R // 2
+def all_reduce(M, OUT, T, R0, R1, R2, send, recv, pos, core):
+    half = M.shape[0] // 2
+    parts = parts_of(half)
     pend = []
-    other = dev(pos, 1 - core)
-    n = [0]
     def copy(src, dst, to):
-        i = n[0]; n[0] += 1
+        i = len(pend)
         c = pltpu.make_async_remote_copy(src, dst, send.at[i], recv.at[i], device_id=to, device_id_type=MESH)
         c.start(); pend.append(c); return c
-    mine = pl.ds(pl.multiple_of(core * half, 8), half)
-    theirs = pl.ds(pl.multiple_of((1 - core) * half, 8), half)
-    first = copy(M.at[theirs], T.at[4], other)
-    first.wait_recv()
-    T[0] = M[mine] + T[4]
-    P = parts_of(half)
+    def part(cc, r):
+        return pl.ds(pl.multiple_of(cc * half + r[0], 8), r[1] - r[0])
+    def steps(p, k):
+        d = DIMS[p][k]
+        return pos[d], [(o, j) for o in ((2, 1, 3, 0) if k != 1 else (2, 1, 3)) for j in ((0, 1) if k != 1 else (0,)) if o or j], d
     got = {}
-    def sends(p, k):
-        d = DIMS[p][k]
-        me = pos[d]
-        rr = rows(P[p])
-        RB[k, me, rr] = T[k, rr]
-        for off in (2, 1, 3):
-            got[p, k, off] = copy(T.at[k, rr], RB.at[k, me, rr], dev(moved(pos, d, off), core))
-    for p in range(3):
-        sends(p, 0)
+    def send_step(p, k):
+        me, moves, d = steps(p, k)
+        rr = rows(parts[p])
+        slot = me * 2 + core if k == 0 else me if k == 1 else core * 4 + me
+        buf = (R0, R1, R2)[k]
+        buf[slot, rr] = M[part(core, parts[p])] if k == 0 else T[k - 1, rr]
+        for o, j in moves:
+            to = 1 - core if j else core
+            src = M.at[part(to, parts[p])] if k == 0 else T.at[k - 1, rr]
+            got[p, k, o, j] = copy(src, buf.at[slot, rr], dev(moved(pos, d, o), to))
+    def take(p, k):
+        for o, j in reversed(steps(p, k)[1]):
+            got[p, k, o, j].wait_recv()
+    def quad(buf, i, rr):
+        return (buf[i, rr] + buf[i + 1, rr]) + (buf[i + 2, rr] + buf[i + 3, rr])
+    for p in range(3):
+        send_step(p, 0)
     for k in range(3):
         for p in range(3):
-            rr = rows(P[p])
-            for off in (1, 3, 2):
-                got[p, k, off].wait_recv()
-            T[k + 1, rr] = (RB[k, 0, rr] + RB[k, 1, rr]) + (RB[k, 2, rr] + RB[k, 3, rr])
+            rr = rows(parts[p])
+            take(p, k)
+            if k == 0:
+                T[0, rr] = quad(R0, 0, rr) + quad(R0, 4, rr)
+            elif k == 1:
+                T[1, rr] = quad(R1, 0, rr)
+            else:
+                for h in range(2):
+                    OUT[pl.ds(h * half + parts[p][0], parts[p][1] - parts[p][0])] = quad(R2, 4 * h, rr)
             if k < 2:
-                sends(p, k + 1)
-    c = copy(T.at[3], T.at[5], other)
-    M[mine] = T[3]
-    c.wait_recv()
-    first.wait_send()
-    M[theirs] = T[5]
-    for c in pend[1:]:
+                send_step(p, k + 1)
+    for c in pend:
         c.wait_send()
-    assert n[0] == NG
-
-NG = 29
+    assert len(pend) == NG, len(pend)
+
+NG = 51
 def AR_SCRATCH(R):
-    return [pltpu.VMEM((6, R // 2, 128), F32), pltpu.VMEM((3, 4, R // 2, 128), F32),
+    return [pltpu.VMEM((R, 128), F32), pltpu.VMEM((2, R // 2, 128), F32), pltpu.VMEM((8, R // 2, 128), F32),
+            pltpu.VMEM((4, R // 2, 128), F32), pltpu.VMEM((8, R // 2, 128), F32),
             pltpu.SemaphoreType.DMA((NG,)), pltpu.SemaphoreType.DMA((NG,))]
 
 def gram(a, b):
     return lax.dot_general(a, b, (((0,), (0,)), ((), ())), precision=lax.Precision.HIGHEST, preferred_element_type=F32)
 
-def rs_kernel(m, proj, tab, d_ref, prior, image, grams, H, W, Q, FA, FB, FC, SA, SB, SC, send, recv, T, RB, gsend, grecv):
+def rs_kernel(m, proj, tab, d_ref, prior, image, grams, H, W, Q, FA, FB, FC, SA, SB, SC, send, recv, M, T, R0, R1, R2, gsend, grecv):
     pos, core = coords()
-    barrier_all(pos, core, True)
-    total, finish = reduce_scatter(proj, tab, H, W, Q, (FA, FB, FC), (SA, SB, SC), send, recv, pos, core)
+    entered = barrier_all(pos, core)
+    total, finish = reduce_scatter(proj, tab, H, W, Q, (FA, FB, FC), (SA, SB, SC), send, recv, pos, core, entered)
     for b in range(5):
         rr = pl.ds(b * 128, 128)
         image[rr] = prior[rr] * d_ref[rr] + total(b * 128, b * 128 + 128).T
-    grams[pl.ds(0, 128)] = gram(d_ref[...], image[...])
+    M[pl.ds(0, 128)] = gram(d_ref[...], image[...])
     if m > 1:
-        grams[pl.ds(128, 128)] = gram(image[...], image[...])
-        grams[pl.ds(256, 128)] = gram(d_ref[...], d_ref[...])
-    all_reduce(grams, T, RB, gsend, grecv, pos, core)
+        M[pl.ds(128, 128)] = gram(image[...], image[...])
+        M[pl.ds(256, 128)] = gram(d_ref[...], d_ref[...])
+    all_reduce(M, grams, T, R0, R1, R2, gsend, grecv, pos, core)
     finish()
 
 def rs_call(m, proj, tab, d, prior):
@@ -380,7 +399,7 @@
         out_shape=(jax.ShapeDtypeStruct((640, 128), F32), jax.ShapeDtypeStruct((128 * m, 128), F32)),
         in_specs=[V, pl.BlockSpec(memory_space=pltpu.SMEM), V, V], out_specs=(V, V),
         scratch_shapes=RS_SCRATCH(BF16, F32) + AR_SCRATCH(128 * m),
-        compiler_params=pltpu.CompilerParams(collective_id=1 + m, has_side_effects=True, vmem_limit_bytes=34 << 20),
+        compiler_params=pltpu.CompilerParams(collective_id=1 + m, has_side_effects=True, vmem_limit_bytes=36 << 20),
     )(proj, tab, d, prior)
 
 F32, BF16 = jnp.float32, jnp.bfloat16
@@ -394,10 +413,11 @@
     pos, core = coords()
     lp = pltpu.make_async_copy(panel_h, panel, lsem.at[0])
     lf = pltpu.make_async_copy(fac_h, fac, lsem.at[1])
+    entered = entry_barrier(pos, core)
+    lp.start(); lf.start()
     for b in range(5):
         G[pos[0], pos[1], pos[2], core, pl.ds(b * 128, 128)] = v_ref[pl.ds(b * 128, 128)].T.astype(BF16)
-    entry_barrier(pos, core)
-    lp.start(); lf.start()
+    entered()
     n = gather_all(G, send, recv, csend, crecv, pos, core)
     assert n == (NS, NC), n
     proj[256] = jnp.zeros((128, 128), BF16)

time: 286 us -> 285 us (level)
  no operation moved by 1% of the time
where the time goes in v4:
time: 285 us
  Pallas kernels  279 us (98%)
  local copies, waits for them, and re-layouts  3.02 us (1%)
    pallas_call x2, Pallas kernels, rs_call(): pl.pallas_call(functools.partial(rs_kernel, m), out_shape=(jax.ShapeDtype...  130 us
    pallas_call x2, Pallas kernels, k1_call(): pl.pallas_call(k1_kernel, out_shape=jax.ShapeDtypeStruct((257, 128, 128),...  120 us
    pallas_call x1, Pallas kernels, first_call(): pl.pallas_call(first_kernel, out_shape=(big, big, big, small), in_specs=[...  14.9 us
    pallas_call x1, Pallas kernels, last_call(): pl.pallas_call(last_kernel, out_shape=(big, big), in_specs=[V] * 6, out_s...  13.8 us

profile of v4, /device:TPU:1, one launch (start us, length us, event | category | flops | bytes accessed | tf_op | source)
XLA Modules:
  0.0 284.6 jit_solution(3960453600680796792)
XLA Ops:
  0.6 0.9 multiply_add_fusion
  1.5 0.8 broadcast_in_dim.63.prior
  2.4 0.3 copy.10
  2.7 0.5 reshape.91
  3.2 0.4 select_reduce_fusion.1
  3.7 0.2 copy.11
  3.9 0.2 reshape.93.tab
  4.1 0.0 copy-start
  4.1 1.0 copy-done
  5.1 0.0 copy-start.1
  5.1 63.1 %shard_map.77.proj = bf16[257,128,128]{2,1,0:T(8,128)(2,1)S(1)} custom-call(f32[640,128]{1,0:T(8,128)S(1)} %bitcast.8, s32[128]{0:T(128)S(1)} %get-tuple-element.27.idx_ref, bf16[16,256,1024]{2,1,0:T(8,128)(2,1)} %panel_h.3, bf16[16,256,256]{2,1,0:T(8,128)(2,1)} %fac_h.3), custom_call_target="tpu_custom_call" | custom-call | tf_op jit(solution)/shard_map/pallas_call | solution.py:448
  68.2 0.0 copy-done.1
  68.2 66.9 %shard_map.78 = (f32[640,128]{1,0:T(8,128)S(1)}, f32[384,128]{1,0:T(8,128)S(1)}) custom-call(bf16[257,128,128]{2,1,0:T(8,128)(2,1)S(1)} %shard_map.77.proj, s32[2560]{0:T(1024)S(1)} %reshape.93.tab, f32[640,128]{1,0:T(8,128)S(1)} %bitcast.9, f32[640,128]{1,0:T(8,128)S(1)} %broadcast_in_dim.63.prior), custom_call_target="tpu_custom_call" | custom-call | tf_op jit(solution)/shard_map/pallas_call | solution.py:398
  135.2 14.9 %shard_map.79 = (f32[640,128]{1,0:T(8,128)S(1)}, f32[640,128]{1,0:T(8,128)S(1)}, f32[640,128]{1,0:T(8,128)S(1)}, f32[128,128]{1,0:T(8,128)S(1)}) custom-call(f32[384,128]{1,0:T(8,128)S(1)} %get-tuple-element.12.grams, f32[640,128]{1,0:T(8,128)S(1)} %bitcast.10, f32[640,128]{1,0:T(8,128)S(1)} %get-tuple-element.13.image), custom_call_target="tpu_custom_call" | custom-call | tf_op jit(solution)/shard_map/pallas_call | solution.py:520
  150.1 57.3 %shard_map.80.proj = bf16[257,128,128]{2,1,0:T(8,128)(2,1)S(1)} custom-call(f32[640,128]{1,0:T(8,128)S(1)} %get-tuple-element.14.v_ref.d_ref.d, s32[128]{0:T(128)S(1)} %get-tuple-element.27.idx_ref, bf16[16,256,1024]{2,1,0:T(8,128)(2,1)} %panel_h.3, bf16[16,256,256]{2,1,0:T(8,128)(2,1)} %fac_h.3), custom_call_target="tpu_custom_call" | custom-call | tf_op jit(solution)/shard_map/pallas_call | solution.py:448
  207.4 63.4 %shard_map.81 = (f32[640,128]{1,0:T(8,128)S(1)}, f32[128,128]{1,0:T(8,128)S(1)}) custom-call(bf16[257,128,128]{2,1,0:T(8,128)(2,1)S(1)} %shard_map.80.proj, s32[2560]{0:T(1024)S(1)} %reshape.93.tab, f32[640,128]{1,0:T(8,128)S(1)} %get-tuple-element.14.v_ref.d_ref.d, f32[640,128]{1,0:T(8,128)S(1)} %broadcast_in_dim.63.prior), custom_call_target="tpu_custom_call" | custom-call | tf_op jit(solution)/shard_map/pallas_call | solution.py:398
  270.8 13.8 %shard_map.82 = (f32[640,128]{1,0:T(8,128)}, f32[640,128]{1,0:T(8,128)}) custom-call(f32[128,128]{1,0:T(8,128)S(1)} %get-tuple-element.15.c, f32[128,128]{1,0:T(8,128)S(1)} %get-tuple-element.16.new, f32[640,128]{1,0:T(8,128)S(1)} %get-tuple-element.17.x0, f32[640,128]{1,0:T(8,128)S(1)} %get-tuple-element.18.r0, ...), custom_call_target="tpu_custom_call" | custom-call | tf_op jit(solution)/shard_map/pallas_call | solution.py:526
  (6 shorter events, 0.0 us)
Async XLA Ops:
  4.1 1.0 copy-start
  5.1 63.1 %copy-start.1 = (f32[5,128,128]{2,1,0:T(8,128)S(1)}, f32[5,128,128]{2,1,0:T(8,128)}, u32[]{:S(2)}) copy-start(f32[5,128,128]{2,1,0:T(8,128)} %param.6) | copy-start | bytes 983044

commit v5 on v4

--- a/solution.py
+++ b/solution.py
@@ -459,37 +459,38 @@
 def hdot(a, b, ca=1):
     return lax.dot_general(a, b, (((ca,), (0,)), ((), ())), precision=lax.Precision.HIGHEST, preferred_element_type=F32)
 
+PIV = 16
 def negated_inverses(mats):
-    lane = lax.broadcasted_iota(jnp.int32, (8, 128), 1)
-    sub = lax.broadcasted_iota(jnp.int32, (8, 128), 0)
+    lane = lax.broadcasted_iota(jnp.int32, (PIV, 128), 1)
+    sub = lax.broadcasted_iota(jnp.int32, (PIV, 128), 0)
     wide = lax.broadcasted_iota(jnp.int32, (128, 128), 1)
     def sweep(_, carry):
         out = []
-        tops = [a[:8] for a in carry]
+        tops = [a[:PIV] for a in carry]
         ws = list(tops)
-        for j in range(0, 8, 2):
+        for j in range(0, PIV, 2):
             for m in range(len(ws)):
                 w = ws[m]
-                col0 = jnp.broadcast_to(w[:, j:j + 1], (8, 128))
-                col1 = jnp.broadcast_to(w[:, j + 1:j + 2], (8, 128))
-                row0 = jnp.where(lane == j, 1.0, jnp.where(lane == j + 1, 0.0, jnp.broadcast_to(w[j:j + 1, :], (8, 128))))
-                row1 = jnp.where(lane == j + 1, 1.0, jnp.where(lane == j, 0.0, jnp.broadcast_to(w[j + 1:j + 2, :], (8, 128))))
-                a00 = jnp.broadcast_to(col0[j:j + 1, :], (8, 128))
-                a10 = jnp.broadcast_to(col0[j + 1:j + 2, :], (8, 128))
-                a01 = jnp.broadcast_to(col1[j:j + 1, :], (8, 128))
-                a11 = jnp.broadcast_to(col1[j + 1:j + 2, :], (8, 128))
+                col0 = jnp.broadcast_to(w[:, j:j + 1], (PIV, 128))
+                col1 = jnp.broadcast_to(w[:, j + 1:j + 2], (PIV, 128))
+                row0 = jnp.where(lane == j, 1.0, jnp.where(lane == j + 1, 0.0, jnp.broadcast_to(w[j:j + 1, :], (PIV, 128))))
+                row1 = jnp.where(lane == j + 1, 1.0, jnp.where(lane == j, 0.0, jnp.broadcast_to(w[j + 1:j + 2, :], (PIV, 128))))
+                a00 = jnp.broadcast_to(col0[j:j + 1, :], (PIV, 128))
+                a10 = jnp.broadcast_to(col0[j + 1:j + 2, :], (PIV, 128))
+                a01 = jnp.broadcast_to(col1[j:j + 1, :], (PIV, 128))
+                a11 = jnp.broadcast_to(col1[j + 1:j + 2, :], (PIV, 128))
                 inv = 1.0 / (a00 * a11 - a01 * a10)
                 new0 = (a11 * row0 - a01 * row1) * inv
                 new1 = (a00 * row1 - a10 * row0) * inv
                 w = jnp.where((lane == j) | (lane == j + 1), 0.0, w) - col0 * new0 - col1 * new1
                 ws[m] = jnp.where(sub == j, new0, jnp.where(sub == j + 1, new1, w))
         for a, p, w in zip(carry, tops, ws):
-            m = hdot(jnp.where(lane < 8, 0.0, p), w, 0)
-            rest = jnp.where(wide < 8, m, a - m)
-            first = jnp.where(lane < 8, -w, w)
-            out.append(pltpu.roll(jnp.concatenate([rest[8:], first], axis=0), 120, 1))
+            m = hdot(jnp.where(lane < PIV, 0.0, p), w, 0)
+            rest = jnp.where(wide < PIV, m, a - m)
+            first = jnp.where(lane < PIV, -w, w)
+            out.append(pltpu.roll(jnp.concatenate([rest[PIV:], first], axis=0), 128 - PIV, 1))
         return tuple(out)
-    return lax.fori_loop(0, 16, sweep, tuple(mats))
+    return lax.fori_loop(0, 128 // PIV, sweep, tuple(mats))
 
 def sym(a):
     return (a + a.T) * 0.5

time: 285 us -> 281 us (0.986)
  Pallas kernels: 279 us -> 276 us
where the time goes in v5:
time: 281 us
  Pallas kernels  276 us (98%)
  local copies, waits for them, and re-layouts  3.02 us (1%)
    pallas_call x2, Pallas kernels, rs_call(): pl.pallas_call(functools.partial(rs_kernel, m), out_shape=(jax.ShapeDtype...  130 us
    pallas_call x2, Pallas kernels, k1_call(): pl.pallas_call(k1_kernel, out_shape=jax.ShapeDtypeStruct((257, 128, 128),...  120 us
    pallas_call x1, Pallas kernels, first_call(): pl.pallas_call(first_kernel, out_shape=(big, big, big, small), in_specs=[...  12.9 us
    pallas_call x1, Pallas kernels, last_call(): pl.pallas_call(last_kernel, out_shape=(big, big), in_specs=[V] * 6, out_s...  12.3 us

profile of v5, /device:TPU:1, one launch (start us, length us, event | category | flops | bytes accessed | tf_op | source)
XLA Modules:
  0.0 281.1 jit_solution(6890811806386440970)
XLA Ops:
  0.6 0.9 multiply_add_fusion
  1.5 0.8 broadcast_in_dim.63.prior
  2.4 0.3 copy.10
  2.7 0.5 reshape.91
  3.2 0.4 select_reduce_fusion.1
  3.7 0.2 copy.11
  3.9 0.2 reshape.93.tab
  4.1 0.0 copy-start
  4.1 1.0 copy-done
  5.1 0.0 copy-start.1
  5.1 63.1 %shard_map.77.proj = bf16[257,128,128]{2,1,0:T(8,128)(2,1)S(1)} custom-call(f32[640,128]{1,0:T(8,128)S(1)} %bitcast.8, s32[128]{0:T(128)S(1)} %get-tuple-element.27.idx_ref, bf16[16,256,1024]{2,1,0:T(8,128)(2,1)} %panel_h.3, bf16[16,256,256]{2,1,0:T(8,128)(2,1)} %fac_h.3), custom_call_target="tpu_custom_call" | custom-call | tf_op jit(solution)/shard_map/pallas_call | solution.py:448
  68.2 0.0 copy-done.1
  68.2 66.9 %shard_map.78 = (f32[640,128]{1,0:T(8,128)S(1)}, f32[384,128]{1,0:T(8,128)S(1)}) custom-call(bf16[257,128,128]{2,1,0:T(8,128)(2,1)S(1)} %shard_map.77.proj, s32[2560]{0:T(1024)S(1)} %reshape.93.tab, f32[640,128]{1,0:T(8,128)S(1)} %bitcast.9, f32[640,128]{1,0:T(8,128)S(1)} %broadcast_in_dim.63.prior), custom_call_target="tpu_custom_call" | custom-call | tf_op jit(solution)/shard_map/pallas_call | solution.py:398
  135.2 12.9 %shard_map.79 = (f32[640,128]{1,0:T(8,128)S(1)}, f32[640,128]{1,0:T(8,128)S(1)}, f32[640,128]{1,0:T(8,128)S(1)}, f32[128,128]{1,0:T(8,128)S(1)}) custom-call(f32[384,128]{1,0:T(8,128)S(1)} %get-tuple-element.12.grams, f32[640,128]{1,0:T(8,128)S(1)} %bitcast.10, f32[640,128]{1,0:T(8,128)S(1)} %get-tuple-element.13.image), custom_call_target="tpu_custom_call" | custom-call | tf_op jit(solution)/shard_map/pallas_call | solution.py:521
  148.1 57.3 %shard_map.80.proj = bf16[257,128,128]{2,1,0:T(8,128)(2,1)S(1)} custom-call(f32[640,128]{1,0:T(8,128)S(1)} %get-tuple-element.14.v_ref.d_ref.d, s32[128]{0:T(128)S(1)} %get-tuple-element.27.idx_ref, bf16[16,256,1024]{2,1,0:T(8,128)(2,1)} %panel_h.3, bf16[16,256,256]{2,1,0:T(8,128)(2,1)} %fac_h.3), custom_call_target="tpu_custom_call" | custom-call | tf_op jit(solution)/shard_map/pallas_call | solution.py:448
  205.4 63.5 %shard_map.81 = (f32[640,128]{1,0:T(8,128)S(1)}, f32[128,128]{1,0:T(8,128)S(1)}) custom-call(bf16[257,128,128]{2,1,0:T(8,128)(2,1)S(1)} %shard_map.80.proj, s32[2560]{0:T(1024)S(1)} %reshape.93.tab, f32[640,128]{1,0:T(8,128)S(1)} %get-tuple-element.14.v_ref.d_ref.d, f32[640,128]{1,0:T(8,128)S(1)} %broadcast_in_dim.63.prior), custom_call_target="tpu_custom_call" | custom-call | tf_op jit(solution)/shard_map/pallas_call | solution.py:398
  268.9 12.3 %shard_map.82 = (f32[640,128]{1,0:T(8,128)}, f32[640,128]{1,0:T(8,128)}) custom-call(f32[128,128]{1,0:T(8,128)S(1)} %get-tuple-element.15.c, f32[128,128]{1,0:T(8,128)S(1)} %get-tuple-element.16.new, f32[640,128]{1,0:T(8,128)S(1)} %get-tuple-element.17.x0, f32[640,128]{1,0:T(8,128)S(1)} %get-tuple-element.18.r0, ...), custom_call_target="tpu_custom_call" | custom-call | tf_op jit(solution)/shard_map/pallas_call | solution.py:527
  (6 shorter events, 0.0 us)
Async XLA Ops:
  4.1 1.0 copy-start
  5.1 63.1 %copy-start.1 = (f32[5,128,128]{2,1,0:T(8,128)S(1)}, f32[5,128,128]{2,1,0:T(8,128)}, u32[]{:S(2)}) copy-start(f32[5,128,128]{2,1,0:T(8,128)} %param.6) | copy-start | bytes 983044
